TPU v7x, 256 devices: a whole 4x4x8 slice. The times are simulated.
256 devices in a mesh: gx: 4 (over x), gy: 8 (over z_hi, core), gz: 8 (over y, z_lo).
Axes of the slice: x: 4, y: 4, z: 8 (z_hi: 4, z_lo: 2; z = z_hi * 2 + z_lo), core: 2. Of those that a mesh axis runs over, the one named last changes fastest.
Arguments:
- state: float32 [7, 4, 8, 65536], P(None, 'gx', 'gy', 'gz'), as said below
- tile_lists: int32 [4, 8, 512, 8], P('gx', 'gy', 'gz'), may hold values from 0 to 63
- tile_counts: int32 [4, 8, 512], P('gx', 'gy', 'gz'), may hold values from 1 to 8, as said below
- ghost_counts: int32 [4, 8, 8, 4], P('gx', 'gy', 'gz'), may hold values from 1 to 12
- cell_index: int32 [4, 8, 65536], P('gx', 'gy', 'gz'), may hold values from 0 to 8191, as said below
- fluid_vel: float32 [3, 4, 8, 8192], P(None, 'gx', 'gy', 'gz'), may hold values from -6 to 6
- fluid_frac: float32 [4, 8, 8192], P('gx', 'gy', 'gz'), may hold values from 0.4 to 0.9
Outputs:
- velocity_new: float32 [3, 4, 8, 65536], P(None, 'gx', 'gy', 'gz')
- fluid_new: float32 [3, 4, 8, 8192], P(None, 'gx', 'gy', 'gz')
Inputs may be any that keep to these rules, and one draw needn't show every extreme that they name: `state`: rows 0 to 2 are positions within 0 to 1, rows 3 to 5 velocities, row 6 radii within 0.15 to 0.35. `tile_counts`: in every box the first tile's count is the largest of that box. `cell_index`: A particle of box z along z has its cell in that box's slab, cells z * 1024 to (z + 1) * 1024 - 1, or in the slab of a box beside it along z.
All inputs are finite; a program needn't handle non-finite values.
Results may differ from a plain program's by a relative error of at most 0.0003.
Values sent between devices are 32-bit elements; how exact they have to be, the bound alone decides.
A program may use at most 64 MiB of HBM per device.

v0:
```python
import jax
import jax.numpy as jnp
from jax import lax
from jax.sharding import PartitionSpec as P

TILE = 128
K = 8
NT = 64
GB = 12


stiffness = 5.0
damping = 2.0
time_step = 0.25
drag_coef = 64.0
fluid_density = 2.0
radius_ref = 0.25
highest = lax.Precision.HIGHEST


def passed_along(value, axis, steps):
    count = lax.axis_size(axis)
    first, last = (max(0, -steps), min(count, count - steps))
    return lax.ppermute(value, axis, [(source, source + steps) for source in range(first, last)])


def padded(shard, sides, width):
    for axis, dim in sides:
        devices, length = (lax.axis_size(axis), shard.shape[dim])
        up = [(i, (i + 1) % devices) for i in range(devices - 1)]
        down = [(j, i) for i, j in up]
        last = lax.slice_in_dim(shard, length - width, length, axis=dim)
        first = lax.slice_in_dim(shard, 0, width, axis=dim)
        before = lax.ppermute(last, axis, up)
        after = lax.ppermute(first, axis, down)
        shard = jnp.concatenate([before, shard, after], axis=dim)
    return shard


def pair_weight(near_tiles, far_tiles):
    offset = near_tiles[0][:, :, None] - far_tiles[0][:, None, :]
    distance = offset * offset
    for column in range(1, 3):
        offset = near_tiles[column][:, :, None] - far_tiles[column][:, None, :]
        distance = distance + offset * offset
    contact_reach = near_tiles[6][:, :, None] + far_tiles[6][:, None, :]
    return (
        jnp.maximum(contact_reach * contact_reach - distance, 0.0)
        * near_tiles[7][:, :, None]
        * far_tiles[7][:, None, :]
    )


def force_near(near_tiles, far_tiles, weight):
    totals = jnp.sum(weight, axis=2)
    weighted = jnp.einsum("tij,ctj->cti", weight, far_tiles[0:6], precision=highest)
    return stiffness * (near_tiles[0:3] * totals - weighted[0:3]) - damping * (
        near_tiles[3:6] * totals - weighted[3:6]
    )


def border_face(owned_tiles, ghost_count, face_index):
    border = owned_tiles[0:7, face_index * GB : (face_index + 1) * GB]
    living = (jnp.arange(GB, dtype=jnp.int32) < ghost_count[face_index]).astype(jnp.float32)
    living = jnp.broadcast_to(living[None, :, None], (1, GB, TILE))
    return jnp.concatenate([border, living], axis=0)


def interior_forces(owned_tiles, tile_list, counts):
    blocks = 16
    per_block = NT // blocks

    def one_block(block_index):
        first_tile = block_index * per_block
        near_tiles = lax.dynamic_slice_in_dim(owned_tiles, first_tile, per_block, 1)
        listing = lax.dynamic_slice_in_dim(tile_list, first_tile, per_block, 0)
        counted = lax.dynamic_slice_in_dim(counts, first_tile, per_block, 0)

        def add_listed(listed, running):
            far_tiles = jnp.take(owned_tiles, listing[:, listed], axis=1)
            weight = pair_weight(near_tiles, far_tiles)
            living = (listed < counted).astype(jnp.float32)
            return running + force_near(near_tiles, far_tiles, weight) * living[None, :, None]

        last_listed = K
        return lax.fori_loop(
            0, last_listed, add_listed, jnp.zeros((3, per_block, TILE), jnp.float32)
        )

    pieces = lax.map(one_block, jnp.arange(blocks, dtype=jnp.int32))
    return jnp.moveaxis(pieces, 0, 1).reshape(3, NT, TILE)


def body(state, tile_lists, tile_counts, ghost_counts, cell_index, fluid_vel, fluid_frac):
    particles = state.shape[3]
    cell_count = fluid_vel.shape[3]
    tile_state = state.reshape(7, NT, TILE)
    owned_tiles = jnp.concatenate([tile_state, jnp.ones((1, NT, TILE), jnp.float32)], axis=0)
    tile_list = tile_lists.reshape(NT, K)
    counts = tile_counts.reshape(NT)
    ghost_count = ghost_counts.reshape(4)
    low_x = border_face(owned_tiles, ghost_count, 0)
    high_x = border_face(owned_tiles, ghost_count, 1)
    low_y = border_face(owned_tiles, ghost_count, 2)
    high_y = border_face(owned_tiles, ghost_count, 3)
    fluid_own = fluid_vel.reshape(3, cell_count)
    fraction = fluid_frac.reshape(1, cell_count)
    below_x = passed_along(high_x, "gx", 1)
    above_x = passed_along(low_x, "gx", -1)
    below_y = passed_along(high_y, "gy", 1)
    above_y = passed_along(low_y, "gy", -1)
    face_tiles = jnp.concatenate([low_x, high_x, low_y, high_y], axis=1)
    ghosts = jnp.concatenate([below_x, above_x, below_y, above_y], axis=1)
    across = force_near(face_tiles, ghosts, pair_weight(face_tiles, ghosts))
    interior = interior_forces(owned_tiles, tile_list, counts)
    forces = jnp.concatenate(
        [interior[:, : 4 * GB] + across, interior[:, 4 * GB :]], axis=1
    ).reshape(3, particles)
    velocity = state[3:6].reshape(3, particles)
    radius = state[6].reshape(1, particles)
    masses = (radius / radius_ref) ** 3
    drag_rate = drag_coef * radius * radius
    moved = velocity + time_step * forces / masses
    sources = jnp.concatenate([drag_rate * velocity, drag_rate], axis=0)
    cell_ids = cell_index.reshape(particles)
    first_cell = (lax.axis_index("gz") - 1) * cell_count
    local_ids = cell_ids - first_cell
    partial_value = jax.ops.segment_sum(sources.T, local_ids, num_segments=3 * cell_count).T
    from_above = passed_along(partial_value[:, :cell_count], "gz", -1)
    from_below = passed_along(partial_value[:, 2 * cell_count :], "gz", 1)
    share = partial_value[:, cell_count : 2 * cell_count] + from_above + from_below
    own_new = (fluid_density * fraction * fluid_own + time_step * share[0:3]) / (
        fluid_density * fraction + time_step * share[3:4]
    )
    extended = padded(own_new, (("gz", 1),), cell_count)
    at_cell = jnp.take(extended, local_ids, axis=1)
    coupling = time_step * drag_rate / masses
    velocity_new = (moved + coupling * at_cell) / (1.0 + coupling)
    return (velocity_new.reshape(3, 1, 1, particles), own_new.reshape(3, 1, 1, cell_count))


def solution(mesh):
    return jax.shard_map(
        body,
        mesh=mesh,
        in_specs=(
            P(None, "gx", "gy", "gz"),
            P("gx", "gy", "gz", None),
            P("gx", "gy", "gz"),
            P("gx", "gy", "gz", None),
            P("gx", "gy", "gz"),
            P(None, "gx", "gy", "gz"),
            P("gx", "gy", "gz"),
        ),
        out_specs=(P(None, "gx", "gy", "gz"), P(None, "gx", "gy", "gz")),
        check_vma=False,
    )
```

profile of v0, /device:TPU:95, one launch (start us, length us, event | category | flops | bytes accessed | tf_op | source)
XLA Modules:
  0.0 478.0 jit_solution(16942235375161027408)
XLA Ops:
  15.0 44.7 %scatter_custom_fusion = f32[3072,4]{1,0:T(8,128)S(1)} fusion(s32[8192]{0:T(1024)S(1)} %bitcast.135, f32[8192,4]{1,0:T(8,128)} %copy.54, f32[]{:T(128)} %constant.120.clone.1), kind=kCustom, calls=%fused_computation.55 | custom fusion | flops 32768 | bytes 49664 | tf_op jit(solution)/shard_map/scatter-add | solution.py:128
  77.0 7.8 %collective-permute-start.2 = (f32[8,12,128]{2,0,1:T(8,128)}, f32[8,12,128]{2,0,1:T(8,128)}, u32[]{:S(2)}, u32[]{:S(2)}) collective-permute-start(f32[8,12,128]{2,0,1:T(8,128)} %pad_maximum_fusion.4), channel_id=1, source_target_pairs={{0,8},{8,16},{16,24},{24,32},{32,40},{40,48},{48,56},{1,9},{9,17},... | collective-permute-start | bytes 147464 | tf_op jit(solution)/shard_map/ppermute | solution.py:24
  87.2 298.5 %while.25 = (s32[]{:T(128)}, f32[16,3,4,128]{3,1,2,0:T(4,128)S(1)}, s32[16]{0:T(128)S(1)}, s32[64,8]{0,1:T(8,128)S(1)}, f32[8,64,128]{2,0,1:T(8,128)S(1)}, /*ind...) while((s32[]{:T(128)}, f32[16,3,4,128]{3,1,2,0:T(4,128)S(1)}, ...), condition=%wide.region_4.5_spmd, body=%wide.region_0.4_spmd.sunk | while | flops 6639145 | bytes 271126 | solution.py:90
  88.5 17.3 %while.26 = (s32[]{:T(128)}, f32[3,4,128]{2,0,1:T(4,128)S(1)}, f32[8,4,128]{2,0,1:T(8,128)S(1)}, s32[4,8]{0,1:T(8,128)S(1)}, f32[8,64,128]{2,0,1:T(8,128)S(1)}, /*index=5*/s32[4]{0:T(128)S(1)}, s32[]{:T(128)}, s32[]{:T(128)}) while((s32[]{:T(128)}, f32[3,4,128]{2,0,1:T(4,128)S(1)}, f32[8,4,128]{2,0,1:T(8,128)S(1)}, ...), condition=%wide.region_3.3_spmd.clone, body=%wide.region_1.2_spmd.clone.sunk | while | flops 6639139 | bytes 221415 | solution.py:86
  107.2 17.3 %while.26 = (s32[]{:T(128)}, f32[3,4,128]{2,0,1:T(4,128)S(1)}, f32[8,4,128]{2,0,1:T(8,128)S(1)}, s32[4,8]{0,1:T(8,128)S(1)}, f32[8,64,128]{2,0,1:T(8,128)S(1)}, /*index=5*/s32[4]{0:T(128)S(1)}, s32[]{:T(128)}, s32[]{:T(128)}) while((s32[]{:T(128)}, f32[3,4,128]{2,0,1:T(4,128)S(1)}, f32[8,4,128]{2,0,1:T(8,128)S(1)}, ...), condition=%wide.region_3.3_spmd.clone, body=%wide.region_1.2_spmd.clone.sunk | while | flops 6639139 | bytes 221415 | solution.py:86
  125.8 17.3 %while.26 = (s32[]{:T(128)}, f32[3,4,128]{2,0,1:T(4,128)S(1)}, f32[8,4,128]{2,0,1:T(8,128)S(1)}, s32[4,8]{0,1:T(8,128)S(1)}, f32[8,64,128]{2,0,1:T(8,128)S(1)}, /*index=5*/s32[4]{0:T(128)S(1)}, s32[]{:T(128)}, s32[]{:T(128)}) while((s32[]{:T(128)}, f32[3,4,128]{2,0,1:T(4,128)S(1)}, f32[8,4,128]{2,0,1:T(8,128)S(1)}, ...), condition=%wide.region_3.3_spmd.clone, body=%wide.region_1.2_spmd.clone.sunk | while | flops 6639139 | bytes 221415 | solution.py:86
  144.5 17.3 %while.26 = (s32[]{:T(128)}, f32[3,4,128]{2,0,1:T(4,128)S(1)}, f32[8,4,128]{2,0,1:T(8,128)S(1)}, s32[4,8]{0,1:T(8,128)S(1)}, f32[8,64,128]{2,0,1:T(8,128)S(1)}, /*index=5*/s32[4]{0:T(128)S(1)}, s32[]{:T(128)}, s32[]{:T(128)}) while((s32[]{:T(128)}, f32[3,4,128]{2,0,1:T(4,128)S(1)}, f32[8,4,128]{2,0,1:T(8,128)S(1)}, ...), condition=%wide.region_3.3_spmd.clone, body=%wide.region_1.2_spmd.clone.sunk | while | flops 6639139 | bytes 221415 | solution.py:86
  163.2 17.3 %while.26 = (s32[]{:T(128)}, f32[3,4,128]{2,0,1:T(4,128)S(1)}, f32[8,4,128]{2,0,1:T(8,128)S(1)}, s32[4,8]{0,1:T(8,128)S(1)}, f32[8,64,128]{2,0,1:T(8,128)S(1)}, /*index=5*/s32[4]{0:T(128)S(1)}, s32[]{:T(128)}, s32[]{:T(128)}) while((s32[]{:T(128)}, f32[3,4,128]{2,0,1:T(4,128)S(1)}, f32[8,4,128]{2,0,1:T(8,128)S(1)}, ...), condition=%wide.region_3.3_spmd.clone, body=%wide.region_1.2_spmd.clone.sunk | while | flops 6639139 | bytes 221415 | solution.py:86
  181.8 17.3 %while.26 = (s32[]{:T(128)}, f32[3,4,128]{2,0,1:T(4,128)S(1)}, f32[8,4,128]{2,0,1:T(8,128)S(1)}, s32[4,8]{0,1:T(8,128)S(1)}, f32[8,64,128]{2,0,1:T(8,128)S(1)}, /*index=5*/s32[4]{0:T(128)S(1)}, s32[]{:T(128)}, s32[]{:T(128)}) while((s32[]{:T(128)}, f32[3,4,128]{2,0,1:T(4,128)S(1)}, f32[8,4,128]{2,0,1:T(8,128)S(1)}, ...), condition=%wide.region_3.3_spmd.clone, body=%wide.region_1.2_spmd.clone.sunk | while | flops 6639139 | bytes 221415 | solution.py:86
  200.5 17.3 %while.26 = (s32[]{:T(128)}, f32[3,4,128]{2,0,1:T(4,128)S(1)}, f32[8,4,128]{2,0,1:T(8,128)S(1)}, s32[4,8]{0,1:T(8,128)S(1)}, f32[8,64,128]{2,0,1:T(8,128)S(1)}, /*index=5*/s32[4]{0:T(128)S(1)}, s32[]{:T(128)}, s32[]{:T(128)}) while((s32[]{:T(128)}, f32[3,4,128]{2,0,1:T(4,128)S(1)}, f32[8,4,128]{2,0,1:T(8,128)S(1)}, ...), condition=%wide.region_3.3_spmd.clone, body=%wide.region_1.2_spmd.clone.sunk | while | flops 6639139 | bytes 221415 | solution.py:86
  219.1 17.3 %while.26 = (s32[]{:T(128)}, f32[3,4,128]{2,0,1:T(4,128)S(1)}, f32[8,4,128]{2,0,1:T(8,128)S(1)}, s32[4,8]{0,1:T(8,128)S(1)}, f32[8,64,128]{2,0,1:T(8,128)S(1)}, /*index=5*/s32[4]{0:T(128)S(1)}, s32[]{:T(128)}, s32[]{:T(128)}) while((s32[]{:T(128)}, f32[3,4,128]{2,0,1:T(4,128)S(1)}, f32[8,4,128]{2,0,1:T(8,128)S(1)}, ...), condition=%wide.region_3.3_spmd.clone, body=%wide.region_1.2_spmd.clone.sunk | while | flops 6639139 | bytes 221415 | solution.py:86
  237.8 17.3 %while.26 = (s32[]{:T(128)}, f32[3,4,128]{2,0,1:T(4,128)S(1)}, f32[8,4,128]{2,0,1:T(8,128)S(1)}, s32[4,8]{0,1:T(8,128)S(1)}, f32[8,64,128]{2,0,1:T(8,128)S(1)}, /*index=5*/s32[4]{0:T(128)S(1)}, s32[]{:T(128)}, s32[]{:T(128)}) while((s32[]{:T(128)}, f32[3,4,128]{2,0,1:T(4,128)S(1)}, f32[8,4,128]{2,0,1:T(8,128)S(1)}, ...), condition=%wide.region_3.3_spmd.clone, body=%wide.region_1.2_spmd.clone.sunk | while | flops 6639139 | bytes 221415 | solution.py:86
  256.5 17.3 %while.26 = (s32[]{:T(128)}, f32[3,4,128]{2,0,1:T(4,128)S(1)}, f32[8,4,128]{2,0,1:T(8,128)S(1)}, s32[4,8]{0,1:T(8,128)S(1)}, f32[8,64,128]{2,0,1:T(8,128)S(1)}, /*index=5*/s32[4]{0:T(128)S(1)}, s32[]{:T(128)}, s32[]{:T(128)}) while((s32[]{:T(128)}, f32[3,4,128]{2,0,1:T(4,128)S(1)}, f32[8,4,128]{2,0,1:T(8,128)S(1)}, ...), condition=%wide.region_3.3_spmd.clone, body=%wide.region_1.2_spmd.clone.sunk | while | flops 6639139 | bytes 221415 | solution.py:86
  275.1 17.3 %while.26 = (s32[]{:T(128)}, f32[3,4,128]{2,0,1:T(4,128)S(1)}, f32[8,4,128]{2,0,1:T(8,128)S(1)}, s32[4,8]{0,1:T(8,128)S(1)}, f32[8,64,128]{2,0,1:T(8,128)S(1)}, /*index=5*/s32[4]{0:T(128)S(1)}, s32[]{:T(128)}, s32[]{:T(128)}) while((s32[]{:T(128)}, f32[3,4,128]{2,0,1:T(4,128)S(1)}, f32[8,4,128]{2,0,1:T(8,128)S(1)}, ...), condition=%wide.region_3.3_spmd.clone, body=%wide.region_1.2_spmd.clone.sunk | while | flops 6639139 | bytes 221415 | solution.py:86
  293.8 17.3 %while.26 = (s32[]{:T(128)}, f32[3,4,128]{2,0,1:T(4,128)S(1)}, f32[8,4,128]{2,0,1:T(8,128)S(1)}, s32[4,8]{0,1:T(8,128)S(1)}, f32[8,64,128]{2,0,1:T(8,128)S(1)}, /*index=5*/s32[4]{0:T(128)S(1)}, s32[]{:T(128)}, s32[]{:T(128)}) while((s32[]{:T(128)}, f32[3,4,128]{2,0,1:T(4,128)S(1)}, f32[8,4,128]{2,0,1:T(8,128)S(1)}, ...), condition=%wide.region_3.3_spmd.clone, body=%wide.region_1.2_spmd.clone.sunk | while | flops 6639139 | bytes 221415 | solution.py:86
  312.4 17.3 %while.26 = (s32[]{:T(128)}, f32[3,4,128]{2,0,1:T(4,128)S(1)}, f32[8,4,128]{2,0,1:T(8,128)S(1)}, s32[4,8]{0,1:T(8,128)S(1)}, f32[8,64,128]{2,0,1:T(8,128)S(1)}, /*index=5*/s32[4]{0:T(128)S(1)}, s32[]{:T(128)}, s32[]{:T(128)}) while((s32[]{:T(128)}, f32[3,4,128]{2,0,1:T(4,128)S(1)}, f32[8,4,128]{2,0,1:T(8,128)S(1)}, ...), condition=%wide.region_3.3_spmd.clone, body=%wide.region_1.2_spmd.clone.sunk | while | flops 6639139 | bytes 221415 | solution.py:86
  331.1 17.3 %while.26 = (s32[]{:T(128)}, f32[3,4,128]{2,0,1:T(4,128)S(1)}, f32[8,4,128]{2,0,1:T(8,128)S(1)}, s32[4,8]{0,1:T(8,128)S(1)}, f32[8,64,128]{2,0,1:T(8,128)S(1)}, /*index=5*/s32[4]{0:T(128)S(1)}, s32[]{:T(128)}, s32[]{:T(128)}) while((s32[]{:T(128)}, f32[3,4,128]{2,0,1:T(4,128)S(1)}, f32[8,4,128]{2,0,1:T(8,128)S(1)}, ...), condition=%wide.region_3.3_spmd.clone, body=%wide.region_1.2_spmd.clone.sunk | while | flops 6639139 | bytes 221415 | solution.py:86
  349.7 17.3 %while.26 = (s32[]{:T(128)}, f32[3,4,128]{2,0,1:T(4,128)S(1)}, f32[8,4,128]{2,0,1:T(8,128)S(1)}, s32[4,8]{0,1:T(8,128)S(1)}, f32[8,64,128]{2,0,1:T(8,128)S(1)}, /*index=5*/s32[4]{0:T(128)S(1)}, s32[]{:T(128)}, s32[]{:T(128)}) while((s32[]{:T(128)}, f32[3,4,128]{2,0,1:T(4,128)S(1)}, f32[8,4,128]{2,0,1:T(8,128)S(1)}, ...), condition=%wide.region_3.3_spmd.clone, body=%wide.region_1.2_spmd.clone.sunk | while | flops 6639139 | bytes 221415 | solution.py:86
  368.4 17.3 %while.26 = (s32[]{:T(128)}, f32[3,4,128]{2,0,1:T(4,128)S(1)}, f32[8,4,128]{2,0,1:T(8,128)S(1)}, s32[4,8]{0,1:T(8,128)S(1)}, f32[8,64,128]{2,0,1:T(8,128)S(1)}, /*index=5*/s32[4]{0:T(128)S(1)}, s32[]{:T(128)}, s32[]{:T(128)}) while((s32[]{:T(128)}, f32[3,4,128]{2,0,1:T(4,128)S(1)}, f32[8,4,128]{2,0,1:T(8,128)S(1)}, ...), condition=%wide.region_3.3_spmd.clone, body=%wide.region_1.2_spmd.clone.sunk | while | flops 6639139 | bytes 221415 | solution.py:86
  395.9 7.5 %collective-permute-done.7 = f32[3,1024]{0,1:T(8,128)S(1)} collective-permute-done((f32[3,1024]{0,1:T(8,128)S(1)}, f32[3,1024]{0,1:T(8,128)S(1)}, u32[]{:S(2)}, u32[]{:S(2)}) %collective-permute-start.7) | collective-permute-done | bytes 12320 | tf_op jit(solution)/shard_map/ppermute | solution.py:35
  405.3 8.9 %collective-permute-done.6 = f32[3,1024]{0,1:T(8,128)} collective-permute-done((f32[3,1024]{0,1:T(8,128)S(1)}, f32[3,1024]{0,1:T(8,128)}, u32[]{:S(2)}, u32[]{:S(2)}) %collective-permute-start.6) | collective-permute-done | bytes 12320 | tf_op jit(solution)/shard_map/ppermute | solution.py:34
  415.3 27.7 %gather_fusion.1 = f32[8192,3]{1,0:T(8,128)} fusion(f32[3,3072]{0,1:T(8,128)S(1)} %pad_maximum_fusion, s32[8192]{0:T(1024)S(1)} %broadcast_clamp_fusion), kind=kCustom, calls=%fused_computation.1 | custom fusion | bytes 229376 | tf_op jit(solution)/shard_map/jit(_take)/gather | solution.py:136
  444.8 11.0 %fusion.35 = f32[6,48,128]{2,0,1:T(8,128)S(1)} fusion(f32[48,128]{1,0:T(8,128)S(1)} %bitcast.151, f32[48,128]{1,0:T(8,128)S(1)} %bitcast.141, f32[48,128]{1,0:T(8,128)S(1)} %bitcast.153, f32[48,128]{1,0:T(8,128)S(1)} %bitcast.145, f32[48,128]{1,0:T(8,128)S(1)} %bitcast.155, f32[48,128]{1,0:T(8,128)S(1)} %bitcast.147, f32[48,128]{1,0:T(8,128)S(1)} %bitcast.157, ...), kind=kOutput, calls=%fused_computation.54 | convolution fusion | flops 67633152 | bytes 589824 | tf_op jit(solution)/shard_map/tij,ctj->cti/dot_general | solution.py:56
  464.8 9.7 %fusion.21 = f32[3,1,1,8192]{0,3,2,1:T(8,128)} fusion(f32[8192,3]{1,0:T(8,128)} %gather_fusion.1, f32[3,1,1,8192]{0,3,2,1:T(8,128)} %copy.58, f32[3,1,1,8192]{0,3,2,1:T(8,128)} %copy.51, f32[8192]{0:T(1024)S(1)} %get-tuple-element.251, f32[8192]{0:T(1024)S(1)} %get-tuple-element.252, f32[8192]{0:T(1024)S(1)} %get-tuple-element.250, ...), kind=kLoop, calls=%fused_computation.37 | loop fusion | flops 147456 | bytes 499712 | tf_op jit(solution)/shard_map/div | solution.py:138
  (1462 shorter events, 345.9 us)
Async XLA Ops:
  0.6 4.4 slice-start
  12.1 2.8 copy-start.2
  12.2 54.7 %copy-start.4 = (s32[1,1,1,4]{3,2,1,0:T(1,128)S(1)}, s32[1,1,1,4]{3,2,1,0:T(1,128)}, u32[]{:S(2)}) copy-start(s32[1,1,1,4]{3,2,1,0:T(1,128)} %param.14) | copy-start | bytes 52
  12.2 56.0 %copy-start = (f32[7,1,1,8192]{3,2,1,0:T(1,128)S(1)}, f32[7,1,1,8192]{3,2,1,0:T(1,128)}, u32[]{:S(2)}) copy-start(f32[7,1,1,8192]{3,2,1,0:T(1,128)} %param.11) | copy-start | bytes 688132
  14.9 71.6 %copy-start.5 = (f32[1,1,1024]{2,1,0:T(1,128)S(1)}, f32[1,1,1024]{2,1,0:T(1,128)}, u32[]{:S(2)}) copy-start(f32[1,1,1024]{2,1,0:T(1,128)} %param.17) | copy-start | bytes 12292
  14.9 72.2 %copy-start.1 = (s32[1,1,64,8]{2,3,1,0:T(8,128)S(1)}, s32[1,1,64,8]{2,3,1,0:T(8,128)}, u32[]{:S(2)}) copy-start(s32[1,1,64,8]{2,3,1,0:T(8,128)} %param.12) | copy-start | bytes 6148
  15.0 72.2 %copy-start.6 = (s32[1,1,64]{2,1,0:T(1,128)S(1)}, s32[1,1,64]{2,1,0:T(1,128)}, u32[]{:S(2)}) copy-start(s32[1,1,64]{2,1,0:T(1,128)} %param.13) | copy-start | bytes 772
  60.7 326.2 %collective-permute-start.5 = (f32[4,1024]{0,1:T(8,128)}, f32[4,1024]{0,1:T(8,128)}, u32[]{:S(2)}, u32[]{:S(2)}) collective-permute-start(f32[4,1024]{0,1:T(8,128)} %get-tuple-element.236), channel_id=1, source_target_pairs={{0,1},{1,2},{2,3},{3,4},{4,5},{5,6},{6,7},{8,9},{9,10},{10,11},{11... | collective-permute-start | bytes 49160 | tf_op jit(solution)/shard_map/ppermute | solution.py:24
  64.3 322.7 %collective-permute-start.4 = (f32[4,1024]{0,1:T(8,128)}, f32[4,1024]{0,1:T(8,128)}, u32[]{:S(2)}, u32[]{:S(2)}) collective-permute-start(f32[4,1024]{0,1:T(8,128)} %get-tuple-element.235), channel_id=1, source_target_pairs={{1,0},{2,1},{3,2},{4,3},{5,4},{6,5},{7,6},{9,8},{10,9},{11,10},{12... | collective-permute-start | bytes 49160 | tf_op jit(solution)/shard_map/ppermute | solution.py:24
  68.4 374.7 %collective-permute-start = (f32[8,12,128]{2,0,1:T(8,128)S(1)}, f32[8,12,128]{2,0,1:T(8,128)S(1)}, u32[]{:S(2)}, u32[]{:S(2)}) collective-permute-start(f32[8,12,128]{2,0,1:T(8,128)S(1)} %pad_maximum_fusion.2), channel_id=1, source_target_pairs={{0,64},{64,128},{128,192},{1,65},{65,129},{129,193},{2,66},{66,130... | collective-permute-start | bytes 147464 | tf_op jit(solution)/shard_map/ppermute | solution.py:24
  71.0 372.0 %collective-permute-start.1 = (f32[8,12,128]{2,0,1:T(8,128)}, f32[8,12,128]{2,0,1:T(8,128)}, u32[]{:S(2)}, u32[]{:S(2)}) collective-permute-start(f32[8,12,128]{2,0,1:T(8,128)} %pad_maximum_fusion.1), channel_id=1, source_target_pairs={{64,0},{128,64},{192,128},{65,1},{129,65},{193,129},{66,2},{130,66... | collective-permute-start | bytes 147464 | tf_op jit(solution)/shard_map/ppermute | solution.py:24
  77.0 366.9 %collective-permute-start.2 = (f32[8,12,128]{2,0,1:T(8,128)}, f32[8,12,128]{2,0,1:T(8,128)}, u32[]{:S(2)}, u32[]{:S(2)}) collective-permute-start(f32[8,12,128]{2,0,1:T(8,128)} %pad_maximum_fusion.4), channel_id=1, source_target_pairs={{0,8},{8,16},{16,24},{24,32},{32,40},{40,48},{48,56},{1,9},{9,17},... | collective-permute-start | bytes 147464 | tf_op jit(solution)/shard_map/ppermute | solution.py:24
  87.2 298.6 %copy-start.3 = (f32[3,1,1,1024]{3,2,1,0:T(1,128)S(1)}, f32[3,1,1,1024]{3,2,1,0:T(1,128)}, u32[]{:S(2)}) copy-start(f32[3,1,1,1024]{3,2,1,0:T(1,128)} %param.16) | copy-start | bytes 36868
  389.7 13.7 %collective-permute-start.7 = (f32[3,1024]{0,1:T(8,128)S(1)}, f32[3,1024]{0,1:T(8,128)S(1)}, u32[]{:S(2)}, u32[]{:S(2)}) collective-permute-start(f32[3,1024]{0,1:T(8,128)S(1)} %fusion.41), channel_id=1, source_target_pairs={{1,0},{2,1},{3,2},{4,3},{5,4},{6,5},{7,6},{9,8},{10,9},{11,10},{12... | collective-permute-start | bytes 36872 | tf_op jit(solution)/shard_map/ppermute | solution.py:35
  391.6 22.6 %collective-permute-start.6 = (f32[3,1024]{0,1:T(8,128)S(1)}, f32[3,1024]{0,1:T(8,128)}, u32[]{:S(2)}, u32[]{:S(2)}) collective-permute-start(f32[3,1024]{0,1:T(8,128)S(1)} %fusion.41), channel_id=1, source_target_pairs={{0,1},{1,2},{2,3},{3,4},{4,5},{5,6},{6,7},{8,9},{9,10},{10,11},{11... | collective-permute-start | bytes 36872 | tf_op jit(solution)/shard_map/ppermute | solution.py:34
  403.4 41.3 %collective-permute-start.3 = (f32[8,12,128]{2,0,1:T(8,128)}, f32[8,12,128]{2,0,1:T(8,128)S(1)}, u32[]{:S(2)}, u32[]{:S(2)}) collective-permute-start(f32[8,12,128]{2,0,1:T(8,128)} %pad_maximum_fusion.3), channel_id=1, source_target_pairs={{8,0},{16,8},{24,16},{32,24},{40,32},{48,40},{56,48},{9,1},{17,9},... | collective-permute-start | bytes 147464 | tf_op jit(solution)/shard_map/ppermute | solution.py:24
where the time goes:
time: 479 us; the launch traced here: 478 us
  other arithmetic  166 us (35%)
  local copies, waits for them, and re-layouts  134 us (28%)
  matrix products  119 us (25%)
  starting transfers between devices  27.1 us (6%)
  waiting for transfers between devices  16.4 us (3%)
  loops' own time  13.8 us (3%)
    dot_general x129, matrix products, force_near(): jnp.einsum('tij,ctj->cti', weight, far_tiles[0:6], precision=highest)  119 us
    reduce_sum x129, other arithmetic, force_near(): totals = jnp.sum(weight, axis=2)  74.9 us
    gather x128, local copies, waits for them, and re-layouts, add_listed(): far_tiles = jnp.take(owned_tiles, listing[:, listed], axis=1)  70.5 us
    scatter-add x1, other arithmetic, body(): jax.ops.segment_sum(sources.T, local_ids, num_segments=3 * cell_count)  44.7 us
    gather x1, local copies, waits for them, and re-layouts, body(): at_cell = jnp.take(extended, local_ids, axis=1)  27.7 us
    ppermute x6, starting transfers between devices, passed_along(): lax.ppermute(value, axis, [(source, source + steps) for source in range(f...  21.7 us
    add x128, other arithmetic, add_listed(): running + force_near(near_tiles, far_tiles, weight) * living[None, :, None]  10.6 us
    div x1, other arithmetic, body(): velocity_new = (moved + coupling * at_cell) / (1.0 + coupling)  9.66 us
  transfers between devices with their start and end apart: 8, of which 2 were waited for; matrix products, arithmetic and copies ran while one was open for 68% of the time, Pallas kernels for 0%

commit v1 on v0

v1 whole, which is shorter than its diff:
```python
import functools

import jax
import jax.numpy as jnp
from jax import lax
from jax.experimental import pallas as pl
from jax.experimental.pallas import tpu as pltpu
from jax.sharding import PartitionSpec as P

TILE = 128
K = 8
NT = 64
GB = 12
NB = 4 * GB
HI = 24
ROWS = 8

stiffness = 5.0
damping = 2.0
time_step = 0.25
drag_coef = 64.0
fluid_density = 2.0
radius_ref = 0.25
dead_level = -1.0e4

f32 = jnp.float32
bf16 = jnp.bfloat16
MESH = pl.DeviceIdType.MESH


def rounded(x):
    return x.astype(bf16).astype(f32)


def pieces(x):
    high = rounded(x)
    rest = x - high
    middle = rounded(rest)
    return high, middle, rounded(rest - middle)


def row_iota(shape):
    return lax.broadcasted_iota(jnp.int32, shape, 0)


def build_tile(tile, near_too, v8, table, near, ul):
    block = v8[pl.ds(pl.multiple_of(tile * ROWS, ROWS), ROWS), :]
    row = row_iota((ROWS, TILE))
    high, middle, low = pieces(block)
    shifted_middle = pltpu.roll(middle, 4, 0)
    one = jnp.float32(1.0)
    zero = jnp.float32(0.0)
    tail = jnp.where(row == 5, one, zero)
    far_high = jnp.where(row < 5, high, tail)
    far_middle = jnp.where(row < 5, middle, zero)
    far_low = jnp.where(row < 5, low, zero)
    stack = jnp.concatenate(
        [far_high, far_middle, far_high, far_middle, far_low, far_high] + [jnp.zeros((80, TILE), f32)], axis=0
    )
    table[tile] = stack.T.astype(bf16)
    first = jnp.where(row == 0, one, zero)
    ul[tile] = jnp.where(row >= 5, high, jnp.where((row >= 1) & (row <= 3), shifted_middle, first))
    if near_too:
        mark = jnp.where(row == 4, one, zero)

        def near_form(piece, fill):
            moved = pltpu.roll(piece, 1, 0)
            return jnp.where(row < 4, 2.0 * piece, jnp.where(row == 5, moved, fill))

        near_high = near_form(high, mark)
        near_middle = near_form(middle, zero)
        near_low = near_form(low, zero)
        stack = jnp.concatenate(
            [near_high, near_high, near_middle, near_middle, near_high, near_low] + [jnp.zeros((80, TILE), f32)],
            axis=0,
        )
        near[tile] = stack.astype(bf16)


def pair_sums(far_a, far_b, live_a, live_b, weights, table, ul):
    lhs = jnp.concatenate([table[far_a], table[far_b]], axis=1)
    weight = jnp.maximum(jnp.dot(lhs, weights, preferred_element_type=f32), 0.0)
    high = weight.astype(bf16)
    low = (weight - high.astype(f32)).astype(bf16)
    rows = jnp.concatenate([ul[far_a] * live_a, ul[far_b] * live_b], axis=0).astype(bf16)
    rows = jnp.concatenate([rows, rows], axis=1)
    return jnp.dot(rows, jnp.concatenate([high, low], axis=0), preferred_element_type=f32)


def near_weights(first, near):
    zero = jnp.zeros((TILE, TILE), bf16)
    upper = jnp.concatenate([near[first], zero], axis=1)
    lower = jnp.concatenate([zero, near[first + 1]], axis=1)
    return jnp.concatenate([upper, lower], axis=0)


def kernel(
    sizes,
    lists, counts, ghost_counts, state, cells, fluid_vel, fluid_frac,
    velocity_out, fluid_out,
    v8, send8, table, near, ul, sums, sources, onehot, deposit, slabs, arrived, window, at_cell,
    send_sem, recv_sem,
):
    names = ("gx", "gy", "gz")
    me = {name: lax.axis_index(name) for name in names}

    def beside(name, step):
        count = sizes[name]
        return {name: lax.rem(me[name] + step + count, count)}

    partners = [beside(name, step) for name in names for step in (-1, 1)]
    barrier = pltpu.get_barrier_semaphore()
    for partner in partners:
        pl.semaphore_signal(barrier, inc=1, device_id=partner, device_id_type=MESH)

    def remote(index, source, target, partner):
        return pltpu.make_async_remote_copy(
            src_ref=source, dst_ref=target, send_sem=send_sem.at[index], recv_sem=recv_sem.at[index],
            device_id=partner, device_id_type=MESH,
        )

    radius = state[6]
    masses = radius / radius_ref
    masses = masses * masses * masses
    drag_rate = drag_coef * radius * radius
    level = radius * radius
    for c in range(3):
        centred = state[c] - 0.5
        level = level - centred * centred
        v8[pl.ds(c, NT, stride=ROWS), :] = centred
        v8[pl.ds(5 + c, NT, stride=ROWS), :] = stiffness * centred - damping * state[3 + c]
    v8[pl.ds(3, NT, stride=ROWS), :] = radius
    v8[pl.ds(4, NT, stride=ROWS), :] = level

    row = row_iota((ROWS, TILE))
    for face in range(4):
        def copy_tile(j, carry, face=face):
            tile = face * GB + j
            place = pl.ds(pl.multiple_of(tile * ROWS, ROWS), ROWS)
            living = jnp.where(j < ghost_counts[face], 0.0, dead_level).astype(f32)
            block = v8[place, :]
            send8[place, :] = jnp.where(row == 4, jnp.where(living < -1.0, dead_level, block), block)
            return carry

        lax.fori_loop(0, GB, copy_tile, 0)

    pl.semaphore_wait(barrier, len(partners))

    width = GB * ROWS
    ghost_copies = []
    for face in range(4):
        name = names[face // 2]
        step = -1 if face % 2 == 0 else 1
        opposite = face ^ 1
        ghost_copies.append(
            remote(
                face,
                send8.at[pl.ds(face * width, width), :],
                v8.at[pl.ds(NT * ROWS + opposite * width, width), :],
                beside(name, step),
            )
        )
        ghost_copies[-1].start()

    for c in range(3):
        high = rounded(drag_rate * state[3 + c])
        sources[c] = high
        sources[4 + c] = rounded(drag_rate * state[3 + c] - high)
    high = rounded(drag_rate)
    sources[3] = high
    sources[7] = rounded(drag_rate - high)
    first_cell = (me["gz"] - 1) * (ROWS * TILE)
    step_tiles = 4
    deposit[...] = jnp.zeros_like(deposit)

    def add_chunk(chunk, carry):
        left, right = [], []
        for k in range(step_tiles):
            tile = chunk * step_tiles + k
            local = cells[pl.ds(tile, 1), :] - first_cell
            hot = (row_iota((TILE, TILE)) == (local & (TILE - 1))).astype(f32).astype(bf16)
            onehot[tile] = hot
            right.append(hot)
            mask = row_iota((HI, TILE)) == lax.shift_right_logical(local, 7)
            parts = [jnp.where(mask, sources[q, pl.ds(tile, 1), :], 0.0) for q in range(8)]
            left.append(jnp.concatenate(parts, axis=0).astype(bf16))
        deposit[...] += lax.dot_general(
            jnp.concatenate(left, axis=1), jnp.concatenate(right, axis=1),
            (((1,), (1,)), ((), ())), preferred_element_type=f32,
        )
        return carry

    lax.fori_loop(0, NT // step_tiles, add_chunk, 0)
    for q in range(4):
        both = deposit[pl.ds(q * HI, HI), :] + deposit[pl.ds((4 + q) * HI, HI), :]
        for slab in range(3):
            slabs[slab, q] = both[slab * ROWS:(slab + 1) * ROWS]

    slab_copies = [
        remote(4, slabs.at[0], arrived.at[1], beside("gz", -1)),
        remote(5, slabs.at[2], arrived.at[0], beside("gz", 1)),
    ]
    for copy in slab_copies:
        copy.start()

    def build_own(tile, carry):
        build_tile(tile, True, v8, table, near, ul)
        return carry

    lax.fori_loop(0, NT, build_own, 0)

    def near_pair(pair, carry):
        first = pair * 2
        weights = near_weights(first, near)
        total = jnp.zeros((2 * ROWS, 2 * TILE), f32)
        for s in range(K):
            live_a = jnp.where(s < counts[first], 1.0, 0.0).astype(f32)
            live_b = jnp.where(s < counts[first + 1], 1.0, 0.0).astype(f32)
            total = total + pair_sums(
                lists[first * K + s], lists[(first + 1) * K + s], live_a, live_b, weights, table, ul
            )
        sums[first] = total[0:ROWS, 0:TILE]
        sums[first + 1] = total[ROWS:, TILE:]
        return carry

    half = NT // 4
    lax.fori_loop(0, half, near_pair, 0)

    for copy in slab_copies:
        copy.wait()
    fraction = fluid_density * fluid_frac[...]
    below = fraction + time_step * (slabs[1, 3] + arrived[0, 3] + arrived[1, 3])
    for c in range(3):
        share = slabs[1, c] + arrived[0, c] + arrived[1, c]
        fresh = (fraction * fluid_vel[c] + time_step * share) / below
        window[1, c] = fresh
        fluid_out[c] = fresh
    fluid_copies = [
        remote(6, window.at[1], window.at[2], beside("gz", -1)),
        remote(7, window.at[1], window.at[0], beside("gz", 1)),
    ]
    for copy in fluid_copies:
        copy.start()

    lax.fori_loop(half, NT // 2, near_pair, 0)

    for copy in ghost_copies:
        copy.wait()

    def build_ghost(tile, carry):
        build_tile(NT + tile, False, v8, table, near, ul)
        return carry

    lax.fori_loop(0, NB, build_ghost, 0)
    for face in range(4):
        name = names[face // 2]
        edge = 0 if face % 2 == 0 else sizes[name] - 1
        inside = jnp.where(me[name] == edge, 0, 1)

        def ghost_pair(pair, carry, face=face, inside=inside):
            slot = pair * 2
            first = face * GB + slot
            limit = ghost_counts[face] * inside
            live_a = jnp.where(slot < limit, 1.0, 0.0).astype(f32)
            live_b = jnp.where(slot + 1 < limit, 1.0, 0.0).astype(f32)
            total = pair_sums(NT + first, NT + first + 1, live_a, live_b, near_weights(first, near), table, ul)
            sums[first] += total[0:ROWS, 0:TILE]
            sums[first + 1] += total[ROWS:, TILE:]
            return carry

        lax.fori_loop(0, GB // 2, ghost_pair, 0)

    for copy in fluid_copies:
        copy.wait()
    left = []
    for c in range(3):
        full = jnp.concatenate([window[0, c], window[1, c], window[2, c]], axis=0)
        high = rounded(full)
        left.append(jnp.concatenate([high, rounded(full - high)], axis=1))
    left = jnp.concatenate(left, axis=0).astype(bf16)

    def take_chunk(chunk, carry):
        hots = [onehot[chunk * step_tiles + k] for k in range(step_tiles)]
        hots = jnp.concatenate(hots, axis=1)
        spread = jnp.dot(left, jnp.concatenate([hots, hots], axis=0), preferred_element_type=f32)
        for k in range(step_tiles):
            tile = chunk * step_tiles + k
            local = cells[pl.ds(tile, 1), :] - first_cell
            mask = row_iota((HI, TILE)) == lax.shift_right_logical(local, 7)
            for c in range(3):
                part = jnp.where(mask, spread[c * HI:(c + 1) * HI, k * TILE:(k + 1) * TILE], 0.0)
                at_cell[c, pl.ds(tile, 1), :] = jnp.sum(part, axis=0, keepdims=True)
        return carry

    lax.fori_loop(0, NT // step_tiles, take_chunk, 0)

    coupling = time_step * drag_rate / masses
    per_mass = time_step / masses
    scale = 1.0 / (1.0 + coupling)
    total_weight = sums[:, 0, :]
    for c in range(3):
        speed = stiffness * (state[c] - 0.5) - damping * state[3 + c]
        high = rounded(speed)
        held = high + rounded(speed - high)
        force = held * total_weight - (sums[:, 5 + c, :] + sums[:, 1 + c, :])
        velocity_out[c] = (state[3 + c] + force * per_mass + coupling * at_cell[c]) * scale


def body(sizes, state, tile_lists, tile_counts, ghost_counts, cell_index, fluid_vel, fluid_frac):
    particles = state.shape[3]
    cell_count = fluid_vel.shape[3]
    vmem = pl.BlockSpec(memory_space=pltpu.VMEM)
    smem = pl.BlockSpec(memory_space=pltpu.SMEM)
    velocity, fluid = pl.pallas_call(
        functools.partial(kernel, sizes),
        out_shape=(
            jax.ShapeDtypeStruct((3, NT, TILE), f32),
            jax.ShapeDtypeStruct((3, ROWS, TILE), f32),
        ),
        in_specs=[smem, smem, smem, vmem, vmem, vmem, vmem],
        out_specs=(vmem, vmem),
        scratch_shapes=[
            pltpu.VMEM(((NT + NB) * ROWS, TILE), f32),
            pltpu.VMEM((NB * ROWS, TILE), f32),
            pltpu.VMEM((NT + NB, TILE, TILE), bf16),
            pltpu.VMEM((NT, TILE, TILE), bf16),
            pltpu.VMEM((NT + NB, ROWS, TILE), f32),
            pltpu.VMEM((NT, ROWS, TILE), f32),
            pltpu.VMEM((8, NT, TILE), f32),
            pltpu.VMEM((NT, TILE, TILE), bf16),
            pltpu.VMEM((8 * HI, TILE), f32),
            pltpu.VMEM((3, 4, ROWS, TILE), f32),
            pltpu.VMEM((2, 4, ROWS, TILE), f32),
            pltpu.VMEM((3, 3, ROWS, TILE), f32),
            pltpu.VMEM((3, NT, TILE), f32),
            pltpu.SemaphoreType.DMA((8,)),
            pltpu.SemaphoreType.DMA((8,)),
        ],
        compiler_params=pltpu.CompilerParams(
            collective_id=0, has_side_effects=True, vmem_limit_bytes=48 * 1024 * 1024
        ),
    )(
        tile_lists.reshape(NT * K),
        tile_counts.reshape(NT),
        ghost_counts.reshape(4),
        state.reshape(7, NT, TILE),
        cell_index.reshape(NT, TILE),
        fluid_vel.reshape(3, ROWS, TILE),
        fluid_frac.reshape(ROWS, TILE),
    )
    return velocity.reshape(3, 1, 1, particles), fluid.reshape(3, 1, 1, cell_count)


def solution(mesh):
    sizes = {name: mesh.shape[name] for name in ("gx", "gy", "gz")}
    return jax.shard_map(
        functools.partial(body, sizes),
        mesh=mesh,
        in_specs=(
            P(None, "gx", "gy", "gz"),
            P("gx", "gy", "gz", None),
            P("gx", "gy", "gz"),
            P("gx", "gy", "gz", None),
            P("gx", "gy", "gz"),
            P(None, "gx", "gy", "gz"),
            P("gx", "gy", "gz"),
        ),
        out_specs=(P(None, "gx", "gy", "gz"), P(None, "gx", "gy", "gz")),
        check_vma=False,
    )
```

time: 479 us -> 54.7 us (0.11)
  the two profiles are of different devices: /device:TPU:95 before, /device:TPU:2 now
where the time goes in v1:
time: 54.7 us; the launch traced here: 54.5 us
  Pallas kernels  50.1 us (92%)
  local copies, waits for them, and re-layouts  3.64 us (7%)
  between operations  0.68 us (1%)
    pallas_call x1, Pallas kernels, body(): pl.pallas_call(functools.partial(kernel, sizes), out_shape=(jax.ShapeDtyp...  50.1 us
    unnamed x17, local copies, waits for them, and re-layouts  3.55 us

profile of v1, /device:TPU:2, one launch (start us, length us, event | category | flops | bytes accessed | tf_op | source)
XLA Modules:
  0.0 54.5 jit_solution(13801096337448748909)
XLA Ops:
  0.6 0.0 copy-start.6
  0.6 0.7 %copy-done.6 = s32[1,1,64,8]{2,3,1,0:T(8,128)S(1)} copy-done((s32[1,1,64,8]{2,3,1,0:T(8,128)S(1)}, s32[1,1,64,8]{2,3,1,0:T(8,128)}, u32[]{:S(2)}) %copy-start.6) | copy-done | bytes 2072
  1.3 0.0 copy-start.1
  1.3 0.1 copy.11
  1.4 0.0 copy-start.2
  1.4 0.0 copy-start.3
  1.4 0.0 copy-start.4
  1.4 0.0 copy-start.5
  1.4 0.1 reshape.31.lists
  1.5 0.5 %copy-done.1 = s32[1,1,8192]{2,1,0:T(1,128)S(1)} copy-done((s32[1,1,8192]{2,1,0:T(1,128)S(1)}, s32[1,1,8192]{2,1,0:T(1,128)}, u32[]{:S(2)}) %copy-start.1) | copy-done | bytes 32792
  2.1 0.0 copy-done.2
  2.1 0.0 copy-done.3
  2.1 0.0 copy-done.4
  2.1 0.0 copy-done.5
  2.1 0.0 copy-start
  2.1 0.9 %copy-done = f32[7,1,1,8192]{3,2,1,0:T(1,128)S(1)} copy-done((f32[7,1,1,8192]{3,2,1,0:T(1,128)S(1)}, f32[7,1,1,8192]{3,2,1,0:T(1,128)}, u32[]{:S(2)}) %copy-start) | copy-done | bytes 229400
  3.1 50.1 %shard_map.86 = (f32[3,64,128]{2,1,0:T(8,128)S(1)}, f32[3,8,128]{2,1,0:T(8,128)S(1)}) custom-call(s32[512]{0:T(512)S(1)} %reshape.31.lists, s32[64]{0:T(128)S(1)} %bitcast.16, s32[4]{0:T(128)S(1)} %bitcast.17, f32[7,64,128]{2,1,0:T(8,128)S(1)} %bitcast.10, s32[64,128]{1,0:T(8,128)S(1)} %bitcast.12, f32[3,8,128]{2,1,0:T(8,128)S(1)} %bitcast.13, ...), custom_call_target="tpu_custom_call" | custom-call | tf_op jit(solution)/shard_map/pallas_call | solution.py:314
  53.2 0.6 %copy.16 = f32[3,1,1,8192]{3,2,1,0:T(1,128)} copy(f32[3,1,1,8192]{3,2,1,0:T(1,128)S(1)} %bitcast.11) | data formatting | bytes 196608
  53.9 0.6 %copy.17 = f32[3,1,1,1024]{3,2,1,0:T(1,128)} copy(f32[3,1,1,1024]{3,2,1,0:T(1,128)S(1)} %bitcast.14) | data formatting | bytes 24576
Async XLA Ops:
  0.6 0.7 %copy-start.6 = (s32[1,1,64,8]{2,3,1,0:T(8,128)S(1)}, s32[1,1,64,8]{2,3,1,0:T(8,128)}, u32[]{:S(2)}) copy-start(s32[1,1,64,8]{2,3,1,0:T(8,128)} %param.8) | copy-start | bytes 6148
  1.3 0.8 %copy-start.1 = (s32[1,1,8192]{2,1,0:T(1,128)S(1)}, s32[1,1,8192]{2,1,0:T(1,128)}, u32[]{:S(2)}) copy-start(s32[1,1,8192]{2,1,0:T(1,128)} %param.11) | copy-start | bytes 98308
  1.4 0.7 %copy-start.2 = (f32[3,1,1,1024]{3,2,1,0:T(1,128)S(1)}, f32[3,1,1,1024]{3,2,1,0:T(1,128)}, u32[]{:S(2)}) copy-start(f32[3,1,1,1024]{3,2,1,0:T(1,128)} %param.12) | copy-start | bytes 36868
  1.4 0.7 %copy-start.3 = (f32[1,1,1024]{2,1,0:T(1,128)S(1)}, f32[1,1,1024]{2,1,0:T(1,128)}, u32[]{:S(2)}) copy-start(f32[1,1,1024]{2,1,0:T(1,128)} %param.13) | copy-start | bytes 12292
  1.4 0.7 %copy-start.4 = (s32[1,1,64]{2,1,0:T(1,128)S(1)}, s32[1,1,64]{2,1,0:T(1,128)}, u32[]{:S(2)}) copy-start(s32[1,1,64]{2,1,0:T(1,128)} %param.9) | copy-start | bytes 772
  1.4 0.7 %copy-start.5 = (s32[1,1,1,4]{3,2,1,0:T(1,128)S(1)}, s32[1,1,1,4]{3,2,1,0:T(1,128)}, u32[]{:S(2)}) copy-start(s32[1,1,1,4]{3,2,1,0:T(1,128)} %param.10) | copy-start | bytes 52
  2.1 0.9 %copy-start = (f32[7,1,1,8192]{3,2,1,0:T(1,128)S(1)}, f32[7,1,1,8192]{3,2,1,0:T(1,128)}, u32[]{:S(2)}) copy-start(f32[7,1,1,8192]{3,2,1,0:T(1,128)} %param.7) | copy-start | bytes 688132

commit v2 on v1

--- a/solution.py
+++ b/solution.py
@@ -14,6 +14,9 @@
 NB = 4 * GB
 HI = 24
 ROWS = 8
+DEPTH = 48
+DEAD = NT + NB
+GROUP = 4
 
 stiffness = 5.0
 damping = 2.0
@@ -21,7 +24,7 @@
 drag_coef = 64.0
 fluid_density = 2.0
 radius_ref = 0.25
-dead_level = -1.0e4
+dead_level = -8192.0
 
 f32 = jnp.float32
 bf16 = jnp.bfloat16
@@ -43,62 +46,46 @@
     return lax.broadcasted_iota(jnp.int32, shape, 0)
 
 
-def build_tile(tile, near_too, v8, table, near, ul):
-    block = v8[pl.ds(pl.multiple_of(tile * ROWS, ROWS), ROWS), :]
+def far_form(block):
     row = row_iota((ROWS, TILE))
     high, middle, low = pieces(block)
-    shifted_middle = pltpu.roll(middle, 4, 0)
-    one = jnp.float32(1.0)
-    zero = jnp.float32(0.0)
-    tail = jnp.where(row == 5, one, zero)
-    far_high = jnp.where(row < 5, high, tail)
-    far_middle = jnp.where(row < 5, middle, zero)
-    far_low = jnp.where(row < 5, low, zero)
-    stack = jnp.concatenate(
-        [far_high, far_middle, far_high, far_middle, far_low, far_high] + [jnp.zeros((80, TILE), f32)], axis=0
-    )
-    table[tile] = stack.T.astype(bf16)
-    first = jnp.where(row == 0, one, zero)
-    ul[tile] = jnp.where(row >= 5, high, jnp.where((row >= 1) & (row <= 3), shifted_middle, first))
-    if near_too:
-        mark = jnp.where(row == 4, one, zero)
-
-        def near_form(piece, fill):
-            moved = pltpu.roll(piece, 1, 0)
-            return jnp.where(row < 4, 2.0 * piece, jnp.where(row == 5, moved, fill))
-
-        near_high = near_form(high, mark)
-        near_middle = near_form(middle, zero)
-        near_low = near_form(low, zero)
-        stack = jnp.concatenate(
-            [near_high, near_high, near_middle, near_middle, near_high, near_low] + [jnp.zeros((80, TILE), f32)],
-            axis=0,
-        )
-        near[tile] = stack.astype(bf16)
-
-
-def pair_sums(far_a, far_b, live_a, live_b, weights, table, ul):
-    lhs = jnp.concatenate([table[far_a], table[far_b]], axis=1)
-    weight = jnp.maximum(jnp.dot(lhs, weights, preferred_element_type=f32), 0.0)
-    high = weight.astype(bf16)
-    low = (weight - high.astype(f32)).astype(bf16)
-    rows = jnp.concatenate([ul[far_a] * live_a, ul[far_b] * live_b], axis=0).astype(bf16)
-    rows = jnp.concatenate([rows, rows], axis=1)
-    return jnp.dot(rows, jnp.concatenate([high, low], axis=0), preferred_element_type=f32)
-
-
-def near_weights(first, near):
-    zero = jnp.zeros((TILE, TILE), bf16)
-    upper = jnp.concatenate([near[first], zero], axis=1)
-    lower = jnp.concatenate([zero, near[first + 1]], axis=1)
-    return jnp.concatenate([upper, lower], axis=0)
+    one = jnp.where(row == 5, 1.0, 0.0).astype(f32)
+    high = jnp.where(row < 5, high, one)
+    middle = jnp.where(row < 5, middle, 0.0)
+    low = jnp.where(row < 5, low, 0.0)
+    return jnp.concatenate([high, middle, high, middle, low, high], axis=0).astype(bf16)
+
+
+def near_form(block):
+    row = row_iota((ROWS, TILE))
+    one = jnp.where(row == 4, 1.0, 0.0).astype(f32)
+    high, middle, low = [
+        jnp.where(row < 4, 2.0 * piece, jnp.where(row == 5, pltpu.roll(piece, 1, 0), 0.0)) for piece in pieces(block)
+    ]
+    high = high + one
+    return jnp.concatenate([high, high, middle, middle, high, low], axis=0)
+
+
+def tile_sums(tile, far_tiles, near, far, v8):
+    heights = jnp.concatenate([far[index] for index in far_tiles], axis=1)
+    level = jnp.dot(near[tile][:, 0:DEPTH], heights, preferred_element_type=f32)
+    weight = jnp.maximum(level, 0.0)
+    totals = [None] * 4
+    for s, index in enumerate(far_tiles):
+        part = weight[:, s * TILE:(s + 1) * TILE].reshape(TILE // ROWS, ROWS, TILE)
+        for q in range(4):
+            term = part
+            if q > 0:
+                term = part * v8[pl.ds(index * ROWS + 4 + q, ROWS, stride=0), :][None]
+            totals[q] = term if totals[q] is None else totals[q] + term
+    return [jnp.sum(total.reshape(TILE, TILE), axis=1, keepdims=True) for total in totals]
 
 
 def kernel(
     sizes,
     lists, counts, ghost_counts, state, cells, fluid_vel, fluid_frac,
     velocity_out, fluid_out,
-    v8, send8, table, near, ul, sums, sources, onehot, deposit, slabs, arrived, window, at_cell,
+    v8, send8, got8, near, far, sums, sources, onehot, deposit, slabs, arrived, window, at_cell,
     send_sem, recv_sem,
 ):
     names = ("gx", "gy", "gz")
@@ -132,17 +119,14 @@
     v8[pl.ds(3, NT, stride=ROWS), :] = radius
     v8[pl.ds(4, NT, stride=ROWS), :] = level
 
+    send8[...] = v8[pl.ds(0, NB * ROWS), :]
+    row = row_iota((NB, TILE))
+    limit = jnp.where(row < GB, ghost_counts[0], GB + ghost_counts[1])
+    limit = jnp.where(row < 2 * GB, limit, 2 * GB + ghost_counts[2])
+    limit = jnp.where(row < 3 * GB, limit, 3 * GB + ghost_counts[3])
+    send8[pl.ds(4, NB, stride=ROWS), :] = jnp.where(row < limit, level[0:NB], dead_level)
     row = row_iota((ROWS, TILE))
-    for face in range(4):
-        def copy_tile(j, carry, face=face):
-            tile = face * GB + j
-            place = pl.ds(pl.multiple_of(tile * ROWS, ROWS), ROWS)
-            living = jnp.where(j < ghost_counts[face], 0.0, dead_level).astype(f32)
-            block = v8[place, :]
-            send8[place, :] = jnp.where(row == 4, jnp.where(living < -1.0, dead_level, block), block)
-            return carry
-
-        lax.fori_loop(0, GB, copy_tile, 0)
+    v8[pl.ds(DEAD * ROWS, ROWS), :] = jnp.where(row == 4, dead_level, 0.0).astype(f32)
 
     pl.semaphore_wait(barrier, len(partners))
 
@@ -156,7 +140,7 @@
             remote(
                 face,
                 send8.at[pl.ds(face * width, width), :],
-                v8.at[pl.ds(NT * ROWS + opposite * width, width), :],
+                got8.at[pl.ds(opposite * width, width), :],
                 beside(name, step),
             )
         )
@@ -203,28 +187,40 @@
     for copy in slab_copies:
         copy.start()
 
-    def build_own(tile, carry):
-        build_tile(tile, True, v8, table, near, ul)
-        return carry
-
-    lax.fori_loop(0, NT, build_own, 0)
-
-    def near_pair(pair, carry):
-        first = pair * 2
-        weights = near_weights(first, near)
-        total = jnp.zeros((2 * ROWS, 2 * TILE), f32)
-        for s in range(K):
-            live_a = jnp.where(s < counts[first], 1.0, 0.0).astype(f32)
-            live_b = jnp.where(s < counts[first + 1], 1.0, 0.0).astype(f32)
-            total = total + pair_sums(
-                lists[first * K + s], lists[(first + 1) * K + s], live_a, live_b, weights, table, ul
-            )
-        sums[first] = total[0:ROWS, 0:TILE]
-        sums[first + 1] = total[ROWS:, TILE:]
-        return carry
-
-    half = NT // 4
-    lax.fori_loop(0, half, near_pair, 0)
+    def block_of(tile):
+        return v8[pl.ds(pl.multiple_of(tile * ROWS, ROWS), ROWS), :]
+
+    def build_own(group, carry):
+        for k in range(GROUP):
+            tile = group * GROUP + k
+            block = block_of(tile)
+            far[tile] = far_form(block)
+            near[tile, :, 0:DEPTH] = near_form(block).T.astype(bf16)
+        return carry
+
+    lax.fori_loop(0, NT // GROUP, build_own, 0)
+    far[DEAD] = far_form(block_of(DEAD))
+    lane = lax.broadcasted_iota(jnp.int32, (TILE, TILE), 1)
+
+    def listed(tile):
+        return [jnp.where(s < counts[tile], lists[s, tile], DEAD) for s in range(K)]
+
+    def near_group(group, extra):
+        columns = []
+        for k in range(GROUP):
+            tile = group * GROUP + k
+            columns.append((tile, tile_sums(tile, listed(tile) + extra(group, k), near, far, v8)))
+        for q in range(4):
+            held = sums[q]
+            for tile, column in columns:
+                held = jnp.where(lane == tile, column[q], held)
+            sums[q] = held
+
+    def inner_group(group, carry):
+        near_group(group, lambda group, k: [])
+        return carry
+
+    lax.fori_loop(NB // GROUP, NT // GROUP, inner_group, 0)
 
     for copy in slab_copies:
         copy.wait()
@@ -242,33 +238,36 @@
     for copy in fluid_copies:
         copy.start()
 
-    lax.fori_loop(half, NT // 2, near_pair, 0)
-
     for copy in ghost_copies:
         copy.wait()
 
-    def build_ghost(tile, carry):
-        build_tile(NT + tile, False, v8, table, near, ul)
-        return carry
-
-    lax.fori_loop(0, NB, build_ghost, 0)
+    def build_ghost(group, carry):
+        for k in range(GROUP):
+            slot = pl.multiple_of((group * GROUP + k) * ROWS, ROWS)
+            block = got8[pl.ds(slot, ROWS), :]
+            v8[pl.ds(NT * ROWS + slot, ROWS), :] = block
+            far[NT + group * GROUP + k] = far_form(block)
+        return carry
+
+    lax.fori_loop(0, NB // GROUP, build_ghost, 0)
+
+    def ghost_of(face, inside):
+        def extra(group, k):
+            tile = group * GROUP + k
+            return [jnp.where(tile - face * GB < ghost_counts[face] * inside, NT + tile, DEAD)]
+
+        return extra
+
     for face in range(4):
         name = names[face // 2]
         edge = 0 if face % 2 == 0 else sizes[name] - 1
         inside = jnp.where(me[name] == edge, 0, 1)
 
-        def ghost_pair(pair, carry, face=face, inside=inside):
-            slot = pair * 2
-            first = face * GB + slot
-            limit = ghost_counts[face] * inside
-            live_a = jnp.where(slot < limit, 1.0, 0.0).astype(f32)
-            live_b = jnp.where(slot + 1 < limit, 1.0, 0.0).astype(f32)
-            total = pair_sums(NT + first, NT + first + 1, live_a, live_b, near_weights(first, near), table, ul)
-            sums[first] += total[0:ROWS, 0:TILE]
-            sums[first + 1] += total[ROWS:, TILE:]
+        def border_group(group, carry, face=face, inside=inside):
+            near_group(group, ghost_of(face, inside))
             return carry
 
-        lax.fori_loop(0, GB // 2, ghost_pair, 0)
+        lax.fori_loop(face * GB // GROUP, (face + 1) * GB // GROUP, border_group, 0)
 
     for copy in fluid_copies:
         copy.wait()
@@ -297,12 +296,10 @@
     coupling = time_step * drag_rate / masses
     per_mass = time_step / masses
     scale = 1.0 / (1.0 + coupling)
-    total_weight = sums[:, 0, :]
+    total_weight = sums[0].T[0:NT]
     for c in range(3):
         speed = stiffness * (state[c] - 0.5) - damping * state[3 + c]
-        high = rounded(speed)
-        held = high + rounded(speed - high)
-        force = held * total_weight - (sums[:, 5 + c, :] + sums[:, 1 + c, :])
+        force = speed * total_weight - sums[1 + c].T[0:NT]
         velocity_out[c] = (state[3 + c] + force * per_mass + coupling * at_cell[c]) * scale
 
 
@@ -320,12 +317,12 @@
         in_specs=[smem, smem, smem, vmem, vmem, vmem, vmem],
         out_specs=(vmem, vmem),
         scratch_shapes=[
-            pltpu.VMEM(((NT + NB) * ROWS, TILE), f32),
+            pltpu.VMEM(((DEAD + 1) * ROWS, TILE), f32),
             pltpu.VMEM((NB * ROWS, TILE), f32),
-            pltpu.VMEM((NT + NB, TILE, TILE), bf16),
+            pltpu.VMEM((NB * ROWS, TILE), f32),
             pltpu.VMEM((NT, TILE, TILE), bf16),
-            pltpu.VMEM((NT + NB, ROWS, TILE), f32),
-            pltpu.VMEM((NT, ROWS, TILE), f32),
+            pltpu.VMEM((DEAD + 1, DEPTH, TILE), bf16),
+            pltpu.VMEM((4, TILE, TILE), f32),
             pltpu.VMEM((8, NT, TILE), f32),
             pltpu.VMEM((NT, TILE, TILE), bf16),
             pltpu.VMEM((8 * HI, TILE), f32),
@@ -340,7 +337,7 @@
             collective_id=0, has_side_effects=True, vmem_limit_bytes=48 * 1024 * 1024
         ),
     )(
-        tile_lists.reshape(NT * K),
+        tile_lists.reshape(NT, K).T,
         tile_counts.reshape(NT),
         ghost_counts.reshape(4),
         state.reshape(7, NT, TILE),

time: 54.7 us -> 35.6 us (0.65)
  Pallas kernels: 50.1 us -> 29.6 us
  local copies, waits for them, and re-layouts: 3.64 us -> 5 us
    pallas_call x1, Pallas kernels: 50.1 us -> 29.6 us  [body(): pl.pallas_call(functools.partial(kernel, sizes), out_shape=(jax.ShapeDtyp...]
    unnamed x17 -> x16, local copies, waits for them, and re-layouts: 3.55 us -> 5 us
where the time goes in v2:
time: 35.6 us; the launch traced here: 35.3 us
  Pallas kernels  29.6 us (83%)
  local copies, waits for them, and re-layouts  5 us (14%)
  between operations  0.67 us (2%)
    pallas_call x1, Pallas kernels, body(): pl.pallas_call(functools.partial(kernel, sizes), out_shape=(jax.ShapeDtyp...  29.6 us
    unnamed x16, local copies, waits for them, and re-layouts  5 us

profile of v2, /device:TPU:2, one launch (start us, length us, event | category | flops | bytes accessed | tf_op | source)
XLA Modules:
  0.0 35.3 jit_solution(5298960195910102661)
XLA Ops:
  0.6 0.0 copy-start.2
  0.6 0.0 copy-start.5
  0.7 0.0 copy-start.6
  0.7 0.7 %copy-done.2 = f32[3,1,1,1024]{3,2,1,0:T(1,128)S(1)} copy-done((f32[3,1,1,1024]{3,2,1,0:T(1,128)S(1)}, f32[3,1,1,1024]{3,2,1,0:T(1,128)}, u32[]{:S(2)}) %copy-start.2) | copy-done | bytes 12312
  1.3 0.0 copy-done.5
  1.3 0.0 copy-done.6
  1.3 0.0 copy-start
  1.3 0.9 %copy-done = f32[7,1,1,8192]{3,2,1,0:T(1,128)S(1)} copy-done((f32[7,1,1,8192]{3,2,1,0:T(1,128)S(1)}, f32[7,1,1,8192]{3,2,1,0:T(1,128)}, u32[]{:S(2)}) %copy-start) | copy-done | bytes 229400
  2.3 0.0 copy-start.1
  2.3 0.8 %copy-done.1 = s32[1,1,8192]{2,1,0:T(1,128)S(1)} copy-done((s32[1,1,8192]{2,1,0:T(1,128)S(1)}, s32[1,1,8192]{2,1,0:T(1,128)}, u32[]{:S(2)}) %copy-start.1) | copy-done | bytes 32792
  3.0 0.0 copy-start.3
  3.0 0.7 %copy-done.3 = s32[1,1,64,8]{2,3,1,0:T(8,128)S(1)} copy-done((s32[1,1,64,8]{2,3,1,0:T(8,128)S(1)}, s32[1,1,64,8]{2,3,1,0:T(8,128)}, u32[]{:S(2)}) %copy-start.3) | copy-done | bytes 2072
  3.7 0.0 copy-start.4
  3.7 0.7 %copy-done.4 = f32[1,1,1024]{2,1,0:T(1,128)S(1)} copy-done((f32[1,1,1024]{2,1,0:T(1,128)S(1)}, f32[1,1,1024]{2,1,0:T(1,128)}, u32[]{:S(2)}) %copy-start.4) | copy-done | bytes 4120
  4.4 29.6 %shard_map.86 = (f32[3,64,128]{2,1,0:T(8,128)S(1)}, f32[3,8,128]{2,1,0:T(8,128)S(1)}) custom-call(s32[8,64]{1,0:T(8,128)S(1)} %bitcast.16, s32[64]{0:T(128)S(1)} %bitcast.18, s32[4]{0:T(128)S(1)} %bitcast.19, f32[7,64,128]{2,1,0:T(8,128)S(1)} %bitcast.11, s32[64,128]{1,0:T(8,128)S(1)} %bitcast.13, f32[3,8,128]{2,1,0:T(8,128)S(1)} %bitcast.14, ...), custom_call_target="tpu_custom_call" | custom-call | tf_op jit(solution)/shard_map/pallas_call | solution.py:311
  34.1 0.6 %copy.15 = f32[3,1,1,8192]{3,2,1,0:T(1,128)} copy(f32[3,1,1,8192]{3,2,1,0:T(1,128)S(1)} %bitcast.12) | data formatting | bytes 196608
  34.7 0.6 %copy.16 = f32[3,1,1,1024]{3,2,1,0:T(1,128)} copy(f32[3,1,1,1024]{3,2,1,0:T(1,128)S(1)} %bitcast.15) | data formatting | bytes 24576
Async XLA Ops:
  0.6 0.7 %copy-start.2 = (f32[3,1,1,1024]{3,2,1,0:T(1,128)S(1)}, f32[3,1,1,1024]{3,2,1,0:T(1,128)}, u32[]{:S(2)}) copy-start(f32[3,1,1,1024]{3,2,1,0:T(1,128)} %param.12) | copy-start | bytes 36868
  0.6 0.7 %copy-start.5 = (s32[1,1,64]{2,1,0:T(1,128)S(1)}, s32[1,1,64]{2,1,0:T(1,128)}, u32[]{:S(2)}) copy-start(s32[1,1,64]{2,1,0:T(1,128)} %param.9) | copy-start | bytes 772
  0.7 0.7 %copy-start.6 = (s32[1,1,1,4]{3,2,1,0:T(1,128)S(1)}, s32[1,1,1,4]{3,2,1,0:T(1,128)}, u32[]{:S(2)}) copy-start(s32[1,1,1,4]{3,2,1,0:T(1,128)} %param.10) | copy-start | bytes 52
  1.3 0.9 %copy-start = (f32[7,1,1,8192]{3,2,1,0:T(1,128)S(1)}, f32[7,1,1,8192]{3,2,1,0:T(1,128)}, u32[]{:S(2)}) copy-start(f32[7,1,1,8192]{3,2,1,0:T(1,128)} %param.7) | copy-start | bytes 688132
  2.3 0.8 %copy-start.1 = (s32[1,1,8192]{2,1,0:T(1,128)S(1)}, s32[1,1,8192]{2,1,0:T(1,128)}, u32[]{:S(2)}) copy-start(s32[1,1,8192]{2,1,0:T(1,128)} %param.11) | copy-start | bytes 98308
  3.0 0.7 %copy-start.3 = (s32[1,1,64,8]{2,3,1,0:T(8,128)S(1)}, s32[1,1,64,8]{2,3,1,0:T(8,128)}, u32[]{:S(2)}) copy-start(s32[1,1,64,8]{2,3,1,0:T(8,128)} %param.8) | copy-start | bytes 6148
  3.7 0.7 %copy-start.4 = (f32[1,1,1024]{2,1,0:T(1,128)S(1)}, f32[1,1,1024]{2,1,0:T(1,128)}, u32[]{:S(2)}) copy-start(f32[1,1,1024]{2,1,0:T(1,128)} %param.13) | copy-start | bytes 12292

commit v3 on v2

--- a/solution.py
+++ b/solution.py
@@ -14,9 +14,10 @@
 NB = 4 * GB
 HI = 24
 ROWS = 8
-DEPTH = 48
+DEPTH = 16
 DEAD = NT + NB
 GROUP = 4
+UNROLL = 8
 
 stiffness = 5.0
 damping = 2.0
@@ -37,9 +38,7 @@
 
 def pieces(x):
     high = rounded(x)
-    rest = x - high
-    middle = rounded(rest)
-    return high, middle, rounded(rest - middle)
+    return high, rounded(x - high)
 
 
 def row_iota(shape):
@@ -48,46 +47,64 @@
 
 def far_form(block):
     row = row_iota((ROWS, TILE))
-    high, middle, low = pieces(block)
-    one = jnp.where(row == 5, 1.0, 0.0).astype(f32)
-    high = jnp.where(row < 5, high, one)
-    middle = jnp.where(row < 5, middle, 0.0)
-    low = jnp.where(row < 5, low, 0.0)
-    return jnp.concatenate([high, middle, high, middle, low, high], axis=0).astype(bf16)
+    high, middle = pieces(block)
+    first = jnp.where(row < 4, high, pltpu.roll(middle, 4, 0))
+    second = jnp.where(row < 5, high, jnp.where(row == 5, pltpu.roll(middle, 1, 0), 1.0))
+    return jnp.concatenate([first, second], axis=0).astype(bf16)
 
 
 def near_form(block):
     row = row_iota((ROWS, TILE))
-    one = jnp.where(row == 4, 1.0, 0.0).astype(f32)
-    high, middle, low = [
-        jnp.where(row < 4, 2.0 * piece, jnp.where(row == 5, pltpu.roll(piece, 1, 0), 0.0)) for piece in pieces(block)
-    ]
-    high = high + one
-    return jnp.concatenate([high, high, middle, middle, high, low], axis=0)
-
-
-def tile_sums(tile, far_tiles, near, far, v8):
+    high, middle = pieces(block)
+    first = 2.0 * jnp.where(row < 4, high, pltpu.roll(high, 4, 0))
+    level = jnp.where(row == 6, pltpu.roll(high, 2, 0), pltpu.roll(middle, 3, 0))
+    second = jnp.where(row < 4, 2.0 * middle, jnp.where(row < 6, 1.0, level))
+    return jnp.concatenate([first, second], axis=0)
+
+
+def set_levels(tile, far_tiles, near, far, levels):
     heights = jnp.concatenate([far[index] for index in far_tiles], axis=1)
-    level = jnp.dot(near[tile][:, 0:DEPTH], heights, preferred_element_type=f32)
-    weight = jnp.maximum(level, 0.0)
-    totals = [None] * 4
-    for s, index in enumerate(far_tiles):
-        part = weight[:, s * TILE:(s + 1) * TILE].reshape(TILE // ROWS, ROWS, TILE)
+    width = len(far_tiles) * TILE
+    levels[:, 0:width] = jnp.dot(near[tile][:, 0:DEPTH], heights, preferred_element_type=f32)
+
+
+def add_far(far_tiles, v8, levels, totals):
+    pulls = [[v8[pl.ds(index * ROWS + 5 + c, ROWS, stride=0), :] for c in range(3)] for index in far_tiles]
+    for r in range(0, TILE, ROWS):
+        held = [None] * 4
+        for s, pull in enumerate(pulls):
+            weight = jnp.maximum(levels[r:r + ROWS, s * TILE:(s + 1) * TILE], 0.0)
+            terms = [weight] + [weight * row for row in pull]
+            held = [term if total is None else total + term for total, term in zip(held, terms)]
         for q in range(4):
-            term = part
-            if q > 0:
-                term = part * v8[pl.ds(index * ROWS + 4 + q, ROWS, stride=0), :][None]
-            totals[q] = term if totals[q] is None else totals[q] + term
-    return [jnp.sum(total.reshape(TILE, TILE), axis=1, keepdims=True) for total in totals]
+            totals[q, r:r + ROWS, :] = held[q]
+
+
+def sum_lanes(tile, totals, sums):
+    mask = lax.broadcasted_iota(jnp.int32, (ROWS, TILE), 1) == tile
+    for q in range(4):
+        for r in range(0, TILE, ROWS):
+            column = jnp.sum(totals[q, r:r + ROWS, :], axis=1, keepdims=True)
+            pltpu.store(sums.at[q, r:r + ROWS, :], jnp.broadcast_to(column, (ROWS, TILE)), mask=mask)
 
 
 def kernel(
     sizes,
+    lists_in, counts_in, ghost_counts_in, state_in, cells_in, fluid_vel_in, fluid_frac_in,
+    velocity_out, fluid_out,
     lists, counts, ghost_counts, state, cells, fluid_vel, fluid_frac,
-    velocity_out, fluid_out,
-    v8, send8, got8, near, far, sums, sources, onehot, deposit, slabs, arrived, window, at_cell,
-    send_sem, recv_sem,
+    v8, send8, got8, near, far, levels, totals, sums, sources, onehot, deposit, slabs, arrived, window, at_cell,
+    send_sem, recv_sem, in_sem,
 ):
+    loads = [
+        pltpu.make_async_copy(source, target, in_sem.at[index])
+        for index, (source, target) in enumerate([
+            (state_in, state), (ghost_counts_in, ghost_counts), (cells_in, cells), (lists_in, lists),
+            (counts_in, counts), (fluid_vel_in, fluid_vel), (fluid_frac_in, fluid_frac),
+        ])
+    ]
+    for load in loads:
+        load.start()
     names = ("gx", "gy", "gz")
     me = {name: lax.axis_index(name) for name in names}
 
@@ -106,6 +123,8 @@
             device_id=partner, device_id_type=MESH,
         )
 
+    for load in loads:
+        load.wait()
     radius = state[6]
     masses = radius / radius_ref
     masses = masses * masses * masses
@@ -154,7 +173,7 @@
     sources[3] = high
     sources[7] = rounded(drag_rate - high)
     first_cell = (me["gz"] - 1) * (ROWS * TILE)
-    step_tiles = 4
+    step_tiles = 16
     deposit[...] = jnp.zeros_like(deposit)
 
     def add_chunk(chunk, carry):
@@ -200,27 +219,28 @@
 
     lax.fori_loop(0, NT // GROUP, build_own, 0)
     far[DEAD] = far_form(block_of(DEAD))
-    lane = lax.broadcasted_iota(jnp.int32, (TILE, TILE), 1)
-
     def listed(tile):
         return [jnp.where(s < counts[tile], lists[s, tile], DEAD) for s in range(K)]
 
-    def near_group(group, extra):
-        columns = []
-        for k in range(GROUP):
-            tile = group * GROUP + k
-            columns.append((tile, tile_sums(tile, listed(tile) + extra(group, k), near, far, v8)))
-        for q in range(4):
-            held = sums[q]
-            for tile, column in columns:
-                held = jnp.where(lane == tile, column[q], held)
-            sums[q] = held
-
-    def inner_group(group, carry):
-        near_group(group, lambda group, k: [])
-        return carry
-
-    lax.fori_loop(NB // GROUP, NT // GROUP, inner_group, 0)
+    def sweep(first, last, listing):
+        set_levels(first, listing(first), near, far, levels.at[0])
+        totals[1] = jnp.zeros((4, TILE, TILE), f32)
+
+        def some_tiles(group, carry):
+            for k in range(UNROLL):
+                tile = first + UNROLL * group + k
+                now, later = k % 2, (k + 1) % 2
+                before = tile - 1 if k > 0 else jnp.where(group == 0, -1, tile - 1)
+                after = tile + 1 if k < UNROLL - 1 else jnp.minimum(tile + 1, last - 1)
+                add_far(listing(tile), v8, levels.at[now], totals.at[now])
+                set_levels(after, listing(after), near, far, levels.at[later])
+                sum_lanes(before, totals.at[later], sums)
+            return carry
+
+        lax.fori_loop(0, (last - first) // UNROLL, some_tiles, 0)
+        sum_lanes(last - 1, totals.at[1], sums)
+
+    sweep(NB, NT, listed)
 
     for copy in slab_copies:
         copy.wait()
@@ -250,24 +270,18 @@
         return carry
 
     lax.fori_loop(0, NB // GROUP, build_ghost, 0)
-
-    def ghost_of(face, inside):
-        def extra(group, k):
-            tile = group * GROUP + k
-            return [jnp.where(tile - face * GB < ghost_counts[face] * inside, NT + tile, DEAD)]
-
-        return extra
-
+    limits = []
     for face in range(4):
         name = names[face // 2]
         edge = 0 if face % 2 == 0 else sizes[name] - 1
-        inside = jnp.where(me[name] == edge, 0, 1)
-
-        def border_group(group, carry, face=face, inside=inside):
-            near_group(group, ghost_of(face, inside))
-            return carry
-
-        lax.fori_loop(face * GB // GROUP, (face + 1) * GB // GROUP, border_group, 0)
+        limits.append(face * GB + jnp.where(me[name] == edge, 0, ghost_counts[face]))
+
+    def listed_too(tile):
+        limit = jnp.where(tile < 2 * GB, jnp.where(tile < GB, limits[0], limits[1]),
+                          jnp.where(tile < 3 * GB, limits[2], limits[3]))
+        return listed(tile) + [jnp.where(tile < limit, NT + tile, DEAD)]
+
+    sweep(0, NB, listed_too)
 
     for copy in fluid_copies:
         copy.wait()
@@ -296,10 +310,13 @@
     coupling = time_step * drag_rate / masses
     per_mass = time_step / masses
     scale = 1.0 / (1.0 + coupling)
-    total_weight = sums[0].T[0:NT]
+    def row_form(q):
+        return sums[q].T[0:NT]
+
+    total_weight = row_form(0)
     for c in range(3):
         speed = stiffness * (state[c] - 0.5) - damping * state[3 + c]
-        force = speed * total_weight - sums[1 + c].T[0:NT]
+        force = speed * total_weight - row_form(1 + c)
         velocity_out[c] = (state[3 + c] + force * per_mass + coupling * at_cell[c]) * scale
 
 
@@ -307,21 +324,30 @@
     particles = state.shape[3]
     cell_count = fluid_vel.shape[3]
     vmem = pl.BlockSpec(memory_space=pltpu.VMEM)
-    smem = pl.BlockSpec(memory_space=pltpu.SMEM)
+    hbm = pl.BlockSpec(memory_space=pltpu.HBM)
     velocity, fluid = pl.pallas_call(
         functools.partial(kernel, sizes),
         out_shape=(
             jax.ShapeDtypeStruct((3, NT, TILE), f32),
             jax.ShapeDtypeStruct((3, ROWS, TILE), f32),
         ),
-        in_specs=[smem, smem, smem, vmem, vmem, vmem, vmem],
+        in_specs=[hbm] * 7,
         out_specs=(vmem, vmem),
         scratch_shapes=[
+            pltpu.SMEM((K, NT), jnp.int32),
+            pltpu.SMEM((NT,), jnp.int32),
+            pltpu.SMEM((4,), jnp.int32),
+            pltpu.VMEM((7, NT, TILE), f32),
+            pltpu.VMEM((NT, TILE), jnp.int32),
+            pltpu.VMEM((3, ROWS, TILE), f32),
+            pltpu.VMEM((ROWS, TILE), f32),
             pltpu.VMEM(((DEAD + 1) * ROWS, TILE), f32),
             pltpu.VMEM((NB * ROWS, TILE), f32),
             pltpu.VMEM((NB * ROWS, TILE), f32),
             pltpu.VMEM((NT, TILE, TILE), bf16),
             pltpu.VMEM((DEAD + 1, DEPTH, TILE), bf16),
+            pltpu.VMEM((2, TILE, (K + 1) * TILE), f32),
+            pltpu.VMEM((2, 4, TILE, TILE), f32),
             pltpu.VMEM((4, TILE, TILE), f32),
             pltpu.VMEM((8, NT, TILE), f32),
             pltpu.VMEM((NT, TILE, TILE), bf16),
@@ -332,9 +358,10 @@
             pltpu.VMEM((3, NT, TILE), f32),
             pltpu.SemaphoreType.DMA((8,)),
             pltpu.SemaphoreType.DMA((8,)),
+            pltpu.SemaphoreType.DMA((7,)),
         ],
         compiler_params=pltpu.CompilerParams(
-            collective_id=0, has_side_effects=True, vmem_limit_bytes=48 * 1024 * 1024
+            collective_id=0, has_side_effects=True, vmem_limit_bytes=64 * 1024 * 1024
         ),
     )(
         tile_lists.reshape(NT, K).T,

time: 35.6 us -> 28.4 us (0.80)
  Pallas kernels: 29.6 us -> 25.5 us
  local copies, waits for them, and re-layouts: 5 us -> 2.15 us
    pallas_call x1, Pallas kernels: 29.6 us -> 25.5 us  [body(): pl.pallas_call(functools.partial(kernel, sizes), out_shape=(jax.ShapeDtyp...]
    unnamed x16 -> x4, local copies, waits for them, and re-layouts: 5 us -> 2.15 us
where the time goes in v3:
time: 28.4 us; the launch traced here: 28.3 us
  Pallas kernels  25.5 us (90%)
  local copies, waits for them, and re-layouts  2.15 us (8%)
  between operations  0.65 us (2%)
    pallas_call x1, Pallas kernels, body(): pl.pallas_call(functools.partial(kernel, sizes), out_shape=(jax.ShapeDtyp...  25.5 us
    unnamed x4, local copies, waits for them, and re-layouts  2.15 us

profile of v3, /device:TPU:2, one launch (start us, length us, event | category | flops | bytes accessed | tf_op | source)
XLA Modules:
  0.0 28.3 jit_solution(517756477548005)
XLA Ops:
  0.6 25.5 %shard_map.86 = (f32[3,64,128]{2,1,0:T(8,128)}, f32[3,8,128]{2,1,0:T(8,128)}) custom-call(s32[8,64]{1,0:T(8,128)} %bitcast.16, s32[64]{0:T(128)} %bitcast.18, s32[4]{0:T(128)} %bitcast.19, f32[7,64,128]{2,1,0:T(8,128)} %bitcast.11, s32[64,128]{1,0:T(8,128)} %bitcast.13, f32[3,8,128]{2,1,0:T(8,128)} %bitcast.14, f32[8,128]{1,0:T(8,128)} %bitcast.17), custom_call_target="tpu_custom_call" | custom-call | tf_op jit(solution)/shard_map/pallas_call | solution.py:328
  26.1 0.0 copy-start
  26.1 1.5 %copy.15 = f32[3,1,1,8192]{3,2,1,0:T(1,128)} copy(f32[3,1,1,8192]{3,2,1,0:T(1,128)} %bitcast.12) | data formatting | bytes 196608
  27.7 0.0 copy-done
  27.7 0.6 %copy.16 = f32[3,1,1,1024]{3,2,1,0:T(1,128)} copy(f32[3,1,1,1024]{3,2,1,0:T(1,128)S(1)} %bitcast.15) | data formatting | bytes 24576
Async XLA Ops:
  26.1 1.6 %copy-start = (f32[3,8,128]{2,1,0:T(8,128)S(1)}, f32[3,8,128]{2,1,0:T(8,128)}, u32[]{:S(2)}) copy-start(f32[3,8,128]{2,1,0:T(8,128)} %get-tuple-element.5) | copy-start | bytes 36868

commit v4 on v3

--- a/solution.py
+++ b/solution.py
@@ -65,7 +65,8 @@
 def set_levels(tile, far_tiles, near, far, levels):
     heights = jnp.concatenate([far[index] for index in far_tiles], axis=1)
     width = len(far_tiles) * TILE
-    levels[:, 0:width] = jnp.dot(near[tile][:, 0:DEPTH], heights, preferred_element_type=f32)
+    rows = near[tile][:, 0:DEPTH]
+    levels[:, 0:width] = jnp.dot(rows, heights, preferred_element_type=f32)
 
 
 def add_far(far_tiles, v8, levels, totals):
@@ -147,6 +148,43 @@
     row = row_iota((ROWS, TILE))
     v8[pl.ds(DEAD * ROWS, ROWS), :] = jnp.where(row == 4, dead_level, 0.0).astype(f32)
 
+    for c in range(3):
+        high = rounded(drag_rate * state[3 + c])
+        sources[c] = high
+        sources[4 + c] = rounded(drag_rate * state[3 + c] - high)
+    high = rounded(drag_rate)
+    sources[3] = high
+    sources[7] = rounded(drag_rate - high)
+    first_cell = (me["gz"] - 1) * (ROWS * TILE)
+    step_tiles = 16
+    deposit[...] = jnp.zeros_like(deposit)
+
+    places = row_iota((TILE, TILE)).astype(f32).astype(bf16)
+
+    def add_chunk(chunk, carry):
+        left, right = [], []
+        for k in range(step_tiles):
+            tile = chunk * step_tiles + k
+            local = cells[pl.ds(tile, 1), :] - first_cell
+            low = (local & (TILE - 1)).astype(f32).astype(bf16)
+            hot = jnp.where(places == low, jnp.ones((), bf16), jnp.zeros((), bf16))
+            onehot[tile] = hot
+            right.append(hot)
+            mask = row_iota((HI, TILE)) == lax.shift_right_logical(local, 7)
+            parts = [jnp.where(mask, sources[q, pl.ds(tile, 1), :], 0.0) for q in range(8)]
+            left.append(jnp.concatenate(parts, axis=0).astype(bf16))
+        deposit[...] += lax.dot_general(
+            jnp.concatenate(left, axis=1), jnp.concatenate(right, axis=1),
+            (((1,), (1,)), ((), ())), preferred_element_type=f32,
+        )
+        return carry
+
+    lax.fori_loop(0, NT // step_tiles, add_chunk, 0)
+    for q in range(4):
+        both = deposit[pl.ds(q * HI, HI), :] + deposit[pl.ds((4 + q) * HI, HI), :]
+        for slab in range(3):
+            slabs[slab, q] = both[slab * ROWS:(slab + 1) * ROWS]
+
     pl.semaphore_wait(barrier, len(partners))
 
     width = GB * ROWS
@@ -164,40 +202,6 @@
             )
         )
         ghost_copies[-1].start()
-
-    for c in range(3):
-        high = rounded(drag_rate * state[3 + c])
-        sources[c] = high
-        sources[4 + c] = rounded(drag_rate * state[3 + c] - high)
-    high = rounded(drag_rate)
-    sources[3] = high
-    sources[7] = rounded(drag_rate - high)
-    first_cell = (me["gz"] - 1) * (ROWS * TILE)
-    step_tiles = 16
-    deposit[...] = jnp.zeros_like(deposit)
-
-    def add_chunk(chunk, carry):
-        left, right = [], []
-        for k in range(step_tiles):
-            tile = chunk * step_tiles + k
-            local = cells[pl.ds(tile, 1), :] - first_cell
-            hot = (row_iota((TILE, TILE)) == (local & (TILE - 1))).astype(f32).astype(bf16)
-            onehot[tile] = hot
-            right.append(hot)
-            mask = row_iota((HI, TILE)) == lax.shift_right_logical(local, 7)
-            parts = [jnp.where(mask, sources[q, pl.ds(tile, 1), :], 0.0) for q in range(8)]
-            left.append(jnp.concatenate(parts, axis=0).astype(bf16))
-        deposit[...] += lax.dot_general(
-            jnp.concatenate(left, axis=1), jnp.concatenate(right, axis=1),
-            (((1,), (1,)), ((), ())), preferred_element_type=f32,
-        )
-        return carry
-
-    lax.fori_loop(0, NT // step_tiles, add_chunk, 0)
-    for q in range(4):
-        both = deposit[pl.ds(q * HI, HI), :] + deposit[pl.ds((4 + q) * HI, HI), :]
-        for slab in range(3):
-            slabs[slab, q] = both[slab * ROWS:(slab + 1) * ROWS]
 
     slab_copies = [
         remote(4, slabs.at[0], arrived.at[1], beside("gz", -1)),
@@ -361,16 +365,21 @@
             pltpu.SemaphoreType.DMA((7,)),
         ],
         compiler_params=pltpu.CompilerParams(
-            collective_id=0, has_side_effects=True, vmem_limit_bytes=64 * 1024 * 1024
+            collective_id=0, has_side_effects=True, vmem_limit_bytes=32 * 1024 * 1024
         ),
     )(
-        tile_lists.reshape(NT, K).T,
-        tile_counts.reshape(NT),
-        ghost_counts.reshape(4),
-        state.reshape(7, NT, TILE),
-        cell_index.reshape(NT, TILE),
-        fluid_vel.reshape(3, ROWS, TILE),
-        fluid_frac.reshape(ROWS, TILE),
+        *[
+            pltpu.with_memory_space_constraint(value, pltpu.HBM)
+            for value in (
+                tile_lists.reshape(NT, K).T,
+                tile_counts.reshape(NT),
+                ghost_counts.reshape(4),
+                state.reshape(7, NT, TILE),
+                cell_index.reshape(NT, TILE),
+                fluid_vel.reshape(3, ROWS, TILE),
+                fluid_frac.reshape(ROWS, TILE),
+            )
+        ]
     )
     return velocity.reshape(3, 1, 1, particles), fluid.reshape(3, 1, 1, cell_count)
 

time: 28.4 us -> 25.5 us (0.90)
  Pallas kernels: 25.5 us -> 23.5 us
  local copies, waits for them, and re-layouts: 2.15 us -> 1.24 us
    pallas_call x1, Pallas kernels: 25.5 us -> 23.5 us  [body(): pl.pallas_call(functools.partial(kernel, sizes), out_shape=(jax.ShapeDtyp...]
    unnamed x4 -> x2, local copies, waits for them, and re-layouts: 2.15 us -> 1.24 us
where the time goes in v4:
time: 25.5 us; the launch traced here: 25.3 us
  Pallas kernels  23.5 us (92%)
  local copies, waits for them, and re-layouts  1.24 us (5%)
  between operations  0.64 us (3%)
    pallas_call x1, Pallas kernels, body(): pl.pallas_call(functools.partial(kernel, sizes), out_shape=(jax.ShapeDtyp...  23.5 us
    unnamed x2, local copies, waits for them, and re-layouts  1.24 us

profile of v4, /device:TPU:2, one launch (start us, length us, event | category | flops | bytes accessed | tf_op | source)
XLA Modules:
  0.0 25.3 jit_solution(4071355596315690925)
XLA Ops:
  0.6 23.5 %shard_map.86 = (f32[3,64,128]{2,1,0:T(8,128)S(1)}, f32[3,8,128]{2,1,0:T(8,128)S(1)}) custom-call(s32[8,64]{1,0:T(8,128)} %bitcast.16, s32[64]{0:T(128)} %bitcast.18, s32[4]{0:T(128)} %bitcast.19, f32[7,64,128]{2,1,0:T(8,128)} %bitcast.13, s32[64,128]{1,0:T(8,128)} %bitcast.14, f32[3,8,128]{2,1,0:T(8,128)} %bitcast.15, f32[8,128]{1,0:T(8,128)} %bitcast.17), custom_call_target="tpu_custom_call" | custom-call | tf_op jit(solution)/shard_map/pallas_call | solution.py:332
  24.1 0.6 %copy.15 = f32[3,1,1,8192]{3,2,1,0:T(1,128)} copy(f32[3,1,1,8192]{3,2,1,0:T(1,128)S(1)} %bitcast.11) | data formatting | bytes 196608
  24.7 0.6 %copy.16 = f32[3,1,1,1024]{3,2,1,0:T(1,128)} copy(f32[3,1,1,1024]{3,2,1,0:T(1,128)S(1)} %bitcast.12) | data formatting | bytes 24576

commit v5 on v4

--- a/solution.py
+++ b/solution.py
@@ -92,9 +92,9 @@
 def kernel(
     sizes,
     lists_in, counts_in, ghost_counts_in, state_in, cells_in, fluid_vel_in, fluid_frac_in,
-    velocity_out, fluid_out,
+    base, gain, window_out,
     lists, counts, ghost_counts, state, cells, fluid_vel, fluid_frac,
-    v8, send8, got8, near, far, levels, totals, sums, sources, onehot, deposit, slabs, arrived, window, at_cell,
+    v8, send8, got8, near, far, levels, totals, sums, sources, deposit, slabs, arrived, window,
     send_sem, recv_sem, in_sem,
 ):
     loads = [
@@ -168,7 +168,6 @@
             local = cells[pl.ds(tile, 1), :] - first_cell
             low = (local & (TILE - 1)).astype(f32).astype(bf16)
             hot = jnp.where(places == low, jnp.ones((), bf16), jnp.zeros((), bf16))
-            onehot[tile] = hot
             right.append(hot)
             mask = row_iota((HI, TILE)) == lax.shift_right_logical(local, 7)
             parts = [jnp.where(mask, sources[q, pl.ds(tile, 1), :], 0.0) for q in range(8)]
@@ -254,7 +253,6 @@
         share = slabs[1, c] + arrived[0, c] + arrived[1, c]
         fresh = (fraction * fluid_vel[c] + time_step * share) / below
         window[1, c] = fresh
-        fluid_out[c] = fresh
     fluid_copies = [
         remote(6, window.at[1], window.at[2], beside("gz", -1)),
         remote(7, window.at[1], window.at[0], beside("gz", 1)),
@@ -289,6 +287,23 @@
 
     for copy in fluid_copies:
         copy.wait()
+    coupling = time_step * drag_rate / masses
+    per_mass = time_step / masses
+    scale = 1.0 / (1.0 + coupling)
+    window_out[...] = window[...]
+    gain[...] = coupling * scale
+    total_weight = sums[0].T[0:NT]
+    for c in range(3):
+        speed = stiffness * (state[c] - 0.5) - damping * state[3 + c]
+        force = speed * total_weight - sums[1 + c].T[0:NT]
+        base[c] = (state[3 + c] + force * per_mass) * scale
+
+
+def finish(base, gain, window, cells, velocity_out, fluid_out, at_cell):
+    first_cell = (lax.axis_index("gz") - 1) * (ROWS * TILE)
+    step_tiles = 16
+    fluid_out[...] = window[1]
+    places = row_iota((TILE, TILE)).astype(f32).astype(bf16)
     left = []
     for c in range(3):
         full = jnp.concatenate([window[0, c], window[1, c], window[2, c]], axis=0)
@@ -297,7 +312,10 @@
     left = jnp.concatenate(left, axis=0).astype(bf16)
 
     def take_chunk(chunk, carry):
-        hots = [onehot[chunk * step_tiles + k] for k in range(step_tiles)]
+        hots = []
+        for k in range(step_tiles):
+            low = ((cells[pl.ds(chunk * step_tiles + k, 1), :] - first_cell) & (TILE - 1)).astype(f32).astype(bf16)
+            hots.append(jnp.where(places == low, jnp.ones((), bf16), jnp.zeros((), bf16)))
         hots = jnp.concatenate(hots, axis=1)
         spread = jnp.dot(left, jnp.concatenate([hots, hots], axis=0), preferred_element_type=f32)
         for k in range(step_tiles):
@@ -311,17 +329,8 @@
 
     lax.fori_loop(0, NT // step_tiles, take_chunk, 0)
 
-    coupling = time_step * drag_rate / masses
-    per_mass = time_step / masses
-    scale = 1.0 / (1.0 + coupling)
-    def row_form(q):
-        return sums[q].T[0:NT]
-
-    total_weight = row_form(0)
-    for c in range(3):
-        speed = stiffness * (state[c] - 0.5) - damping * state[3 + c]
-        force = speed * total_weight - row_form(1 + c)
-        velocity_out[c] = (state[3 + c] + force * per_mass + coupling * at_cell[c]) * scale
+    for c in range(3):
+        velocity_out[c] = base[c] + gain[...] * at_cell[c]
 
 
 def body(sizes, state, tile_lists, tile_counts, ghost_counts, cell_index, fluid_vel, fluid_frac):
@@ -329,14 +338,15 @@
     cell_count = fluid_vel.shape[3]
     vmem = pl.BlockSpec(memory_space=pltpu.VMEM)
     hbm = pl.BlockSpec(memory_space=pltpu.HBM)
-    velocity, fluid = pl.pallas_call(
+    base, gain, window = pl.pallas_call(
         functools.partial(kernel, sizes),
         out_shape=(
             jax.ShapeDtypeStruct((3, NT, TILE), f32),
-            jax.ShapeDtypeStruct((3, ROWS, TILE), f32),
+            jax.ShapeDtypeStruct((NT, TILE), f32),
+            jax.ShapeDtypeStruct((3, 3, ROWS, TILE), f32),
         ),
         in_specs=[hbm] * 7,
-        out_specs=(vmem, vmem),
+        out_specs=(vmem, vmem, vmem),
         scratch_shapes=[
             pltpu.SMEM((K, NT), jnp.int32),
             pltpu.SMEM((NT,), jnp.int32),
@@ -354,12 +364,10 @@
             pltpu.VMEM((2, 4, TILE, TILE), f32),
             pltpu.VMEM((4, TILE, TILE), f32),
             pltpu.VMEM((8, NT, TILE), f32),
-            pltpu.VMEM((NT, TILE, TILE), bf16),
             pltpu.VMEM((8 * HI, TILE), f32),
             pltpu.VMEM((3, 4, ROWS, TILE), f32),
             pltpu.VMEM((2, 4, ROWS, TILE), f32),
             pltpu.VMEM((3, 3, ROWS, TILE), f32),
-            pltpu.VMEM((3, NT, TILE), f32),
             pltpu.SemaphoreType.DMA((8,)),
             pltpu.SemaphoreType.DMA((8,)),
             pltpu.SemaphoreType.DMA((7,)),
@@ -381,6 +389,17 @@
             )
         ]
     )
+    velocity, fluid = pl.pallas_call(
+        finish,
+        out_shape=(
+            jax.ShapeDtypeStruct((3, NT, TILE), f32),
+            jax.ShapeDtypeStruct((3, ROWS, TILE), f32),
+        ),
+        in_specs=[vmem] * 4,
+        out_specs=(vmem, vmem),
+        scratch_shapes=[pltpu.VMEM((3, NT, TILE), f32)],
+        compiler_params=pltpu.CompilerParams(vmem_limit_bytes=16 * 1024 * 1024),
+    )(base, gain, window, cell_index.reshape(NT, TILE))
     return velocity.reshape(3, 1, 1, particles), fluid.reshape(3, 1, 1, cell_count)
 
 

time: 25.5 us -> 24.9 us (0.976)
  local copies, waits for them, and re-layouts: 1.24 us -> 0.01 us
  Pallas kernels: 23.5 us -> 24.2 us
    pallas_call x0 -> x1, Pallas kernels: none -> 1.96 us  [body(): pl.pallas_call(finish, out_shape=(jax.ShapeDtypeStruct((3, NT, TILE), f32...]
    unnamed x2, local copies, waits for them, and re-layouts: 1.24 us -> 0.01 us
    pallas_call x1, Pallas kernels: 23.5 us -> 22.2 us  [body(): pl.pallas_call(functools.partial(kernel, sizes), out_shape=(jax.ShapeDtyp...]
where the time goes in v5:
time: 24.9 us
  Pallas kernels  24.2 us (97%)
  between operations  0.66 us (3%)
    pallas_call x1, Pallas kernels, body(): pl.pallas_call(functools.partial(kernel, sizes), out_shape=(jax.ShapeDtyp...  22.2 us
    pallas_call x1, Pallas kernels, body(): pl.pallas_call(finish, out_shape=(jax.ShapeDtypeStruct((3, NT, TILE), f32...  1.96 us

profile of v5, /device:TPU:2, one launch (start us, length us, event | category | flops | bytes accessed | tf_op | source)
XLA Modules:
  0.0 24.9 jit_solution(8469228341683325540)
XLA Ops:
  0.6 0.0 copy-start
  0.6 22.2 %shard_map.86 = (f32[3,64,128]{2,1,0:T(8,128)S(1)}, f32[64,128]{1,0:T(8,128)S(1)}, f32[3,3,8,128]{3,2,1,0:T(8,128)S(1)}) custom-call(s32[8,64]{1,0:T(8,128)} %bitcast.15, s32[64]{0:T(128)} %bitcast.17, s32[4]{0:T(128)} %bitcast.18, f32[7,64,128]{2,1,0:T(8,128)} %bitcast.13, s32[64,128]{1,0:T(8,128)} %bitcast.11, f32[3,8,128]{2,1,0:T(8,128)} %bitcast.14, ...), custom_call_target="tpu_custom_call" | custom-call | tf_op jit(solution)/shard_map/pallas_call | solution.py:341
  22.9 0.0 copy-done
  22.9 2.0 %shard_map.87 = (f32[3,64,128]{2,1,0:T(8,128)}, f32[3,8,128]{2,1,0:T(8,128)}) custom-call(f32[3,64,128]{2,1,0:T(8,128)S(1)} %get-tuple-element.7.base, f32[64,128]{1,0:T(8,128)S(1)} %get-tuple-element.8.gain, f32[3,3,8,128]{3,2,1,0:T(8,128)S(1)} %get-tuple-element.9.window, s32[64,128]{1,0:T(8,128)S(1)} %bitcast.12), custom_call_target="tpu_custom_call" | custom-call | tf_op jit(solution)/shard_map/pallas_call | solution.py:392
Async XLA Ops:
  0.6 22.2 %copy-start = (s32[1,1,8192]{2,1,0:T(1,128)S(1)}, s32[1,1,8192]{2,1,0:T(1,128)}, u32[]{:S(2)}) copy-start(s32[1,1,8192]{2,1,0:T(1,128)} %param.11) | copy-start | bytes 98308

commit v6 on v5

--- a/solution.py
+++ b/solution.py
@@ -16,8 +16,8 @@
 ROWS = 8
 DEPTH = 16
 DEAD = NT + NB
-GROUP = 4
-UNROLL = 8
+GROUP = 8
+UNROLL = 16
 
 stiffness = 5.0
 damping = 2.0
@@ -62,10 +62,10 @@
     return jnp.concatenate([first, second], axis=0)
 
 
-def set_levels(tile, far_tiles, near, far, levels):
+def set_levels(tile, far_tiles, far, v8, levels):
+    rows = near_form(v8[pl.ds(pl.multiple_of(tile * ROWS, ROWS), ROWS), :]).T.astype(bf16)
     heights = jnp.concatenate([far[index] for index in far_tiles], axis=1)
     width = len(far_tiles) * TILE
-    rows = near[tile][:, 0:DEPTH]
     levels[:, 0:width] = jnp.dot(rows, heights, preferred_element_type=f32)
 
 
@@ -94,7 +94,7 @@
     lists_in, counts_in, ghost_counts_in, state_in, cells_in, fluid_vel_in, fluid_frac_in,
     base, gain, window_out,
     lists, counts, ghost_counts, state, cells, fluid_vel, fluid_frac,
-    v8, send8, got8, near, far, levels, totals, sums, sources, deposit, slabs, arrived, window,
+    v8, send8, got8, far, levels, totals, sums, sources, deposit, slabs, arrived, window,
     send_sem, recv_sem, in_sem,
 ):
     loads = [
@@ -217,7 +217,6 @@
             tile = group * GROUP + k
             block = block_of(tile)
             far[tile] = far_form(block)
-            near[tile, :, 0:DEPTH] = near_form(block).T.astype(bf16)
         return carry
 
     lax.fori_loop(0, NT // GROUP, build_own, 0)
@@ -226,7 +225,7 @@
         return [jnp.where(s < counts[tile], lists[s, tile], DEAD) for s in range(K)]
 
     def sweep(first, last, listing):
-        set_levels(first, listing(first), near, far, levels.at[0])
+        set_levels(first, listing(first), far, v8, levels.at[0])
         totals[1] = jnp.zeros((4, TILE, TILE), f32)
 
         def some_tiles(group, carry):
@@ -236,7 +235,7 @@
                 before = tile - 1 if k > 0 else jnp.where(group == 0, -1, tile - 1)
                 after = tile + 1 if k < UNROLL - 1 else jnp.minimum(tile + 1, last - 1)
                 add_far(listing(tile), v8, levels.at[now], totals.at[now])
-                set_levels(after, listing(after), near, far, levels.at[later])
+                set_levels(after, listing(after), far, v8, levels.at[later])
                 sum_lanes(before, totals.at[later], sums)
             return carry
 
@@ -358,7 +357,6 @@
             pltpu.VMEM(((DEAD + 1) * ROWS, TILE), f32),
             pltpu.VMEM((NB * ROWS, TILE), f32),
             pltpu.VMEM((NB * ROWS, TILE), f32),
-            pltpu.VMEM((NT, TILE, TILE), bf16),
             pltpu.VMEM((DEAD + 1, DEPTH, TILE), bf16),
             pltpu.VMEM((2, TILE, (K + 1) * TILE), f32),
             pltpu.VMEM((2, 4, TILE, TILE), f32),

time: 24.9 us -> 25.2 us (1.012)
  Pallas kernels: 24.2 us -> 24.5 us
    pallas_call x1, Pallas kernels: 22.2 us -> 22.5 us  [body(): pl.pallas_call(functools.partial(kernel, sizes), out_shape=(jax.ShapeDtyp...]
where the time goes in v6:
time: 25.2 us; the launch traced here: 25.1 us
  Pallas kernels  24.5 us (97%)
  between operations  0.66 us (3%)
    pallas_call x1, Pallas kernels, body(): pl.pallas_call(functools.partial(kernel, sizes), out_shape=(jax.ShapeDtyp...  22.5 us
    pallas_call x1, Pallas kernels, body(): pl.pallas_call(finish, out_shape=(jax.ShapeDtypeStruct((3, NT, TILE), f32...  1.96 us

profile of v6, /device:TPU:2, one launch (start us, length us, event | category | flops | bytes accessed | tf_op | source)
XLA Modules:
  0.0 25.1 jit_solution(17801533608226416376)
XLA Ops:
  0.6 0.0 copy-start
  0.6 22.5 %shard_map.86 = (f32[3,64,128]{2,1,0:T(8,128)S(1)}, f32[64,128]{1,0:T(8,128)S(1)}, f32[3,3,8,128]{3,2,1,0:T(8,128)S(1)}) custom-call(s32[8,64]{1,0:T(8,128)} %bitcast.15, s32[64]{0:T(128)} %bitcast.17, s32[4]{0:T(128)} %bitcast.18, f32[7,64,128]{2,1,0:T(8,128)} %bitcast.13, s32[64,128]{1,0:T(8,128)} %bitcast.11, f32[3,8,128]{2,1,0:T(8,128)} %bitcast.14, ...), custom_call_target="tpu_custom_call" | custom-call | tf_op jit(solution)/shard_map/pallas_call | solution.py:340
  23.2 0.0 copy-done
  23.2 2.0 %shard_map.87 = (f32[3,64,128]{2,1,0:T(8,128)}, f32[3,8,128]{2,1,0:T(8,128)}) custom-call(f32[3,64,128]{2,1,0:T(8,128)S(1)} %get-tuple-element.7.base, f32[64,128]{1,0:T(8,128)S(1)} %get-tuple-element.8.gain, f32[3,3,8,128]{3,2,1,0:T(8,128)S(1)} %get-tuple-element.9.window, s32[64,128]{1,0:T(8,128)S(1)} %bitcast.12), custom_call_target="tpu_custom_call" | custom-call | tf_op jit(solution)/shard_map/pallas_call | solution.py:390
Async XLA Ops:
  0.6 22.5 %copy-start = (s32[1,1,8192]{2,1,0:T(1,128)S(1)}, s32[1,1,8192]{2,1,0:T(1,128)}, u32[]{:S(2)}) copy-start(s32[1,1,8192]{2,1,0:T(1,128)} %param.11) | copy-start | bytes 98308
